TPU v7x, 32 devices: a whole 2x2x4 slice. The times are simulated.
32 devices in a mesh: row: 8 (over z, core), col: 4 (over y, x).
Axes of the slice: x: 2, y: 2, z: 4, core: 2. Of those that a mesh axis runs over, the one named last changes fastest.
Arguments:
- gram: bfloat16 [16384, 16384], P('row', 'col'), as said below
- corr: float32 [16384, 128], P('row'), may hold values from -6 to 6
- beta_start: float32 [16384, 2, 128], P('col'), may hold values from -4 to 4
- lambdas: float32 [2], replicated, may hold values from 0.2 to 0.8
- penalty: float32 [262144], replicated, may hold values from 0.5 to 2
- strong: int32 [16384], P('row'), may hold values from 0 to 262143
- active: int32 [2, 8], replicated, may hold values 0 or 1
- order: int32 [8], replicated, may hold values from 0 to 7, each once
Outputs:
- beta: float32 [16384, 2, 128], P('col')
- grad: float32 [16384, 2, 128], P('row')
Inputs may be any that keep to these rules, and one draw needn't show every extreme that they name: `order`: a permutation of the block numbers. `gram`: symmetric, positive definite, diagonal entries of order one.
All inputs are finite; a program needn't handle non-finite values.
Results may differ from a plain program's by a relative error of at most 0.0046.
Values may be sent and summed in bfloat16 or wider, within the bound.
No kernel may reach another device: no remote copies, remote signals or barrier semaphores. Data moves between devices by JAX's collectives and lax.ppermute only.
A program may use at most 128 MiB of HBM per device.

v0:
```python
import jax
import jax.numpy as jnp
from jax import lax
from jax.sharding import PartitionSpec as P


def broadcast(block, axis, source):
    block = jnp.where(lax.axis_index(axis) == source, block, jnp.zeros_like(block))
    return lax.psum(block, axis)


def per_device(gram, corr, beta_start, lambdas, penalty, strong, active, order):
    blk_width = corr.shape[0]
    slot_count = gram.shape[1] // blk_width
    lam_count = beta_start.shape[1]
    phenos = beta_start.shape[2]
    col_index = lax.axis_index("col")
    row_index = lax.axis_index("row")
    beta_round = beta_start.astype(jnp.bfloat16).reshape(slot_count * blk_width, lam_count * phenos)
    partial_value = jnp.dot(gram, beta_round, preferred_element_type=jnp.float32)
    summed = lax.psum(partial_value, "col")
    grad = corr[:, None, :] - summed.reshape(blk_width, lam_count, phenos)
    diag_slots = jnp.stack(
        [
            jnp.diagonal(gram[:, slot * blk_width : (slot + 1) * blk_width])
            for slot in range(slot_count)
        ]
    ).astype(jnp.float32)
    thresh = lambdas[None, :] * penalty[strong][:, None]
    beta = beta_start.reshape(slot_count, blk_width, lam_count, phenos)

    def visit(turn, carry):
        beta, grad = carry
        block = order[turn]
        slot = block % slot_count
        owner_col = block // slot_count
        on_diag = (row_index == block) & (col_index == owner_col)
        in_col = col_index == owner_col
        beta_old = lax.dynamic_index_in_dim(beta, slot, 0, keepdims=False)
        diag_now = lax.dynamic_index_in_dim(diag_slots, slot, 0, keepdims=False)
        diag_safe = jnp.where(on_diag, diag_now, 1.0)[:, None, None]
        shifted = diag_safe * beta_old + grad
        beta_new = (
            jnp.sign(shifted) * jnp.maximum(jnp.abs(shifted) - thresh[:, :, None], 0.0) / diag_safe
        )
        active_now = lax.dynamic_index_in_dim(active, block, 1, keepdims=False)
        beta_new = jnp.where(active_now[None, :, None] == 1, beta_new, beta_old)
        step_bf = (beta_new - beta_old).astype(jnp.bfloat16)
        gram_cols = lax.dynamic_slice_in_dim(gram, slot * blk_width, blk_width, 1)
        arrived = broadcast(step_bf, "row", block)
        arrived = jnp.where(in_col, arrived, jnp.zeros_like(arrived))
        change = lax.cond(
            in_col,
            lambda: jnp.dot(
                gram_cols,
                arrived.reshape(blk_width, lam_count * phenos),
                preferred_element_type=jnp.float32,
            ).astype(jnp.bfloat16),
            lambda: jnp.zeros((blk_width, lam_count * phenos), jnp.bfloat16),
        )
        change_all = broadcast(change, "col", owner_col).reshape(blk_width, lam_count, phenos)
        beta = lax.dynamic_update_index_in_dim(
            beta, beta_old + arrived.astype(jnp.float32), slot, 0
        )
        grad = grad - change_all.astype(jnp.float32)
        return (beta, grad)

    beta, grad = lax.fori_loop(0, order.shape[0], visit, (beta, grad))
    return (beta.reshape(slot_count * blk_width, lam_count, phenos), grad)


def solution(mesh):
    in_specs = (P("row", "col"), P("row", None), P("col", None, None), P(), P(), P("row"), P(), P())
    out_specs = (P("col", None, None), P("row", None, None))
    return jax.shard_map(
        per_device, mesh=mesh, in_specs=in_specs, out_specs=out_specs, check_vma=False
    )
```

profile of v0, /device:TPU:8, one launch (start us, length us, event | category | flops | bytes accessed | tf_op | source)
XLA Modules:
  0.0 1292.8 jit_solution(6653117421282686927)
XLA Ops:
  11.5 9.6 fusion.12
  25.2 12.0 fusion.16
  37.3 32.9 %gather_fusion.1 = bf16[2048]{0:T(1024)(128)(2,1)S(1)} fusion(bf16[2048,2048]{1,0:T(8,128)(2,1)} %get-tuple-element.376, s32[2048]{0:T(1024)S(1)} %bitcast.54), kind=kCustom, calls=%fused_computation.1 | custom fusion | bytes 24576 | tf_op jit(solution)/shard_map/jit(diagonal)/cond/branch_0_fun/gather | solution.py:25
  70.2 32.1 %gather_fusion = bf16[2048]{0:T(1024)(128)(2,1)S(1)} fusion(bf16[2048,2048]{1,0:T(8,128)(2,1)} %get-tuple-element.375, s32[2048]{0:T(1024)S(1)} %bitcast.55), kind=kCustom, calls=%fused_computation | custom fusion | bytes 24576 | tf_op jit(solution)/shard_map/jit(diagonal)/cond/branch_0_fun/gather | solution.py:25
  102.4 11.8 gather_fusion.2
  116.8 1168.1 %while.18 = (s32[]{:T(128)}, f32[2,2048,2,128]{3,2,1,0:T(2,128)}, f32[2048,2,128]{2,1,0:T(2,128)S(1)}, s32[8]{0:T(128)S(1)}, s32[]{:T(128)}, /*index=5*/s32[2,8]...) while((s32[]{:T(128)}, f32[2,2048,2,128]{3,2,1,0:T(2,128)}, ...), condition=%wide.region_6.7_spmd.clone, body=%wide.region_1.6_spmd.clone.sunk | while | flops 2158499840 | bytes 46203608 | solution.py:68
  123.1 12.9 broadcast_select_fusion.9
  136.0 59.1 %all-reduce.6.cloned.1.call-done = bf16[2048,2,128]{2,1,0:T(2,128)(2,1)} async-done(((bf16[2048,2,128]{2,1,0:T(2,128)(2,1)}), bf16[2048,2,128]{2,1,0:T(2,128)(2,1)}) %all-reduce.6.cloned.1.call-update) | async-done | bytes 1048592 | tf_op jit(solution)/shard_map/while/body/eval_jaxpr/psum | solution.py:9
  199.3 6.9 conditional.3
  199.3 6.9 fusion.4
  210.7 50.7 %all-reduce.8.cloned.1.call-done = bf16[2048,2,128]{2,1,0:T(2,128)(2,1)} async-done(((bf16[2048,2,128]{2,1,0:T(2,128)(2,1)}), bf16[2048,2,128]{2,1,0:T(2,128)(2,1)}) %all-reduce.8.cloned.1.call-update) | async-done | bytes 1048592 | tf_op jit(solution)/shard_map/while/body/eval_jaxpr/psum | solution.py:9
  269.1 12.9 broadcast_select_fusion.9
  282.1 58.1 %all-reduce.6.cloned.1.call-done = bf16[2048,2,128]{2,1,0:T(2,128)(2,1)} async-done(((bf16[2048,2,128]{2,1,0:T(2,128)(2,1)}), bf16[2048,2,128]{2,1,0:T(2,128)(2,1)}) %all-reduce.6.cloned.1.call-update) | async-done | bytes 1048592 | tf_op jit(solution)/shard_map/while/body/eval_jaxpr/psum | solution.py:9
  348.4 58.8 %all-reduce.8.cloned.1.call-done = bf16[2048,2,128]{2,1,0:T(2,128)(2,1)} async-done(((bf16[2048,2,128]{2,1,0:T(2,128)(2,1)}), bf16[2048,2,128]{2,1,0:T(2,128)(2,1)}) %all-reduce.8.cloned.1.call-update) | async-done | bytes 1048592 | tf_op jit(solution)/shard_map/while/body/eval_jaxpr/psum | solution.py:9
  415.0 12.9 broadcast_select_fusion.9
  428.0 58.1 %all-reduce.6.cloned.1.call-done = bf16[2048,2,128]{2,1,0:T(2,128)(2,1)} async-done(((bf16[2048,2,128]{2,1,0:T(2,128)(2,1)}), bf16[2048,2,128]{2,1,0:T(2,128)(2,1)}) %all-reduce.6.cloned.1.call-update) | async-done | bytes 1048592 | tf_op jit(solution)/shard_map/while/body/eval_jaxpr/psum | solution.py:9
  494.3 59.7 %all-reduce.8.cloned.1.call-done = bf16[2048,2,128]{2,1,0:T(2,128)(2,1)} async-done(((bf16[2048,2,128]{2,1,0:T(2,128)(2,1)}), bf16[2048,2,128]{2,1,0:T(2,128)(2,1)}) %all-reduce.8.cloned.1.call-update) | async-done | bytes 1048592 | tf_op jit(solution)/shard_map/while/body/eval_jaxpr/psum | solution.py:9
  561.8 12.9 broadcast_select_fusion.9
  574.7 58.1 %all-reduce.6.cloned.1.call-done = bf16[2048,2,128]{2,1,0:T(2,128)(2,1)} async-done(((bf16[2048,2,128]{2,1,0:T(2,128)(2,1)}), bf16[2048,2,128]{2,1,0:T(2,128)(2,1)}) %all-reduce.6.cloned.1.call-update) | async-done | bytes 1048592 | tf_op jit(solution)/shard_map/while/body/eval_jaxpr/psum | solution.py:9
  641.1 59.8 %all-reduce.8.cloned.1.call-done = bf16[2048,2,128]{2,1,0:T(2,128)(2,1)} async-done(((bf16[2048,2,128]{2,1,0:T(2,128)(2,1)}), bf16[2048,2,128]{2,1,0:T(2,128)(2,1)}) %all-reduce.8.cloned.1.call-update) | async-done | bytes 1048592 | tf_op jit(solution)/shard_map/while/body/eval_jaxpr/psum | solution.py:9
  708.6 12.9 broadcast_select_fusion.9
  721.5 58.1 %all-reduce.6.cloned.1.call-done = bf16[2048,2,128]{2,1,0:T(2,128)(2,1)} async-done(((bf16[2048,2,128]{2,1,0:T(2,128)(2,1)}), bf16[2048,2,128]{2,1,0:T(2,128)(2,1)}) %all-reduce.6.cloned.1.call-update) | async-done | bytes 1048592 | tf_op jit(solution)/shard_map/while/body/eval_jaxpr/psum | solution.py:9
  787.9 58.8 %all-reduce.8.cloned.1.call-done = bf16[2048,2,128]{2,1,0:T(2,128)(2,1)} async-done(((bf16[2048,2,128]{2,1,0:T(2,128)(2,1)}), bf16[2048,2,128]{2,1,0:T(2,128)(2,1)}) %all-reduce.8.cloned.1.call-update) | async-done | bytes 1048592 | tf_op jit(solution)/shard_map/while/body/eval_jaxpr/psum | solution.py:9
  854.5 12.9 broadcast_select_fusion.9
  867.4 58.1 %all-reduce.6.cloned.1.call-done = bf16[2048,2,128]{2,1,0:T(2,128)(2,1)} async-done(((bf16[2048,2,128]{2,1,0:T(2,128)(2,1)}), bf16[2048,2,128]{2,1,0:T(2,128)(2,1)}) %all-reduce.6.cloned.1.call-update) | async-done | bytes 1048592 | tf_op jit(solution)/shard_map/while/body/eval_jaxpr/psum | solution.py:9
  933.8 58.8 %all-reduce.8.cloned.1.call-done = bf16[2048,2,128]{2,1,0:T(2,128)(2,1)} async-done(((bf16[2048,2,128]{2,1,0:T(2,128)(2,1)}), bf16[2048,2,128]{2,1,0:T(2,128)(2,1)}) %all-reduce.8.cloned.1.call-update) | async-done | bytes 1048592 | tf_op jit(solution)/shard_map/while/body/eval_jaxpr/psum | solution.py:9
  1000.3 12.9 broadcast_select_fusion.9
  1013.3 58.1 %all-reduce.6.cloned.1.call-done = bf16[2048,2,128]{2,1,0:T(2,128)(2,1)} async-done(((bf16[2048,2,128]{2,1,0:T(2,128)(2,1)}), bf16[2048,2,128]{2,1,0:T(2,128)(2,1)}) %all-reduce.6.cloned.1.call-update) | async-done | bytes 1048592 | tf_op jit(solution)/shard_map/while/body/eval_jaxpr/psum | solution.py:9
  1079.6 58.8 %all-reduce.8.cloned.1.call-done = bf16[2048,2,128]{2,1,0:T(2,128)(2,1)} async-done(((bf16[2048,2,128]{2,1,0:T(2,128)(2,1)}), bf16[2048,2,128]{2,1,0:T(2,128)(2,1)}) %all-reduce.8.cloned.1.call-update) | async-done | bytes 1048592 | tf_op jit(solution)/shard_map/while/body/eval_jaxpr/psum | solution.py:9
  1146.2 12.9 broadcast_select_fusion.9
  1159.2 58.1 %all-reduce.6.cloned.1.call-done = bf16[2048,2,128]{2,1,0:T(2,128)(2,1)} async-done(((bf16[2048,2,128]{2,1,0:T(2,128)(2,1)}), bf16[2048,2,128]{2,1,0:T(2,128)(2,1)}) %all-reduce.6.cloned.1.call-update) | async-done | bytes 1048592 | tf_op jit(solution)/shard_map/while/body/eval_jaxpr/psum | solution.py:9
  1232.8 50.7 %all-reduce.8.cloned.1.call-done = bf16[2048,2,128]{2,1,0:T(2,128)(2,1)} async-done(((bf16[2048,2,128]{2,1,0:T(2,128)(2,1)}), bf16[2048,2,128]{2,1,0:T(2,128)(2,1)}) %all-reduce.8.cloned.1.call-update) | async-done | bytes 1048592 | tf_op jit(solution)/shard_map/while/body/eval_jaxpr/psum | solution.py:9
  (137 shorter events, 119.8 us)
Async XLA Ops:
  7.2 95.3 %copy-start = (f32[262144]{0:T(1024)S(1)}, f32[262144]{0:T(1024)}, u32[]{:S(2)}) copy-start(f32[262144]{0:T(1024)} %param.16) | copy-start | bytes 3145732
  7.2 107.1 %all-reduce.4.cloned.1.call-start = ((), (), s32[]{:S(2)}) async-start(), calls=%async_computation | async-start | bytes 4194304 | tf_op jit(solution)/shard_map/psum | solution.py:21
  9.5 2.0 copy-start.2
  70.2 32.1 %copy-start.5 = (s32[2,8]{1,0:T(2,128)S(1)}, s32[2,8]{1,0:T(2,128)}, u32[]{:S(2)}) copy-start(s32[2,8]{1,0:T(2,128)} %param.18) | copy-start | bytes 196
  70.2 32.2 %copy-start.4 = (s32[2048]{0:T(1024)S(1)}, s32[2048]{0:T(1024)}, u32[]{:S(2)}) copy-start(s32[2048]{0:T(1024)} %param.17) | copy-start | bytes 24580
  114.3 2.6 copy-start.3
  114.3 2.6 copy-start.6
  116.8 78.3 %all-reduce.6.cloned.1.call-start = ((), (), s32[]{:S(2)}) async-start(), calls=%async_computation.1 | async-start | bytes 2097152 | tf_op jit(solution)/shard_map/while/body/eval_jaxpr/psum | solution.py:9
  136.0 125.4 %all-reduce.8.cloned.1.call-start = ((), (), s32[]{:S(2)}) async-start(), calls=%async_computation.2 | async-start | bytes 2097152 | tf_op jit(solution)/shard_map/while/body/eval_jaxpr/psum | solution.py:9
  262.9 77.2 %all-reduce.6.cloned.1.call-start = ((), (), s32[]{:S(2)}) async-start(), calls=%async_computation.1 | async-start | bytes 2097152 | tf_op jit(solution)/shard_map/while/body/eval_jaxpr/psum | solution.py:9
  282.0 125.2 %all-reduce.8.cloned.1.call-start = ((), (), s32[]{:S(2)}) async-start(), calls=%async_computation.2 | async-start | bytes 2097152 | tf_op jit(solution)/shard_map/while/body/eval_jaxpr/psum | solution.py:9
  408.8 77.2 %all-reduce.6.cloned.1.call-start = ((), (), s32[]{:S(2)}) async-start(), calls=%async_computation.1 | async-start | bytes 2097152 | tf_op jit(solution)/shard_map/while/body/eval_jaxpr/psum | solution.py:9
  427.9 126.1 %all-reduce.8.cloned.1.call-start = ((), (), s32[]{:S(2)}) async-start(), calls=%async_computation.2 | async-start | bytes 2097152 | tf_op jit(solution)/shard_map/while/body/eval_jaxpr/psum | solution.py:9
  555.5 77.2 %all-reduce.6.cloned.1.call-start = ((), (), s32[]{:S(2)}) async-start(), calls=%async_computation.1 | async-start | bytes 2097152 | tf_op jit(solution)/shard_map/while/body/eval_jaxpr/psum | solution.py:9
  574.7 126.2 %all-reduce.8.cloned.1.call-start = ((), (), s32[]{:S(2)}) async-start(), calls=%async_computation.2 | async-start | bytes 2097152 | tf_op jit(solution)/shard_map/while/body/eval_jaxpr/psum | solution.py:9
  702.3 77.2 %all-reduce.6.cloned.1.call-start = ((), (), s32[]{:S(2)}) async-start(), calls=%async_computation.1 | async-start | bytes 2097152 | tf_op jit(solution)/shard_map/while/body/eval_jaxpr/psum | solution.py:9
  721.5 125.2 %all-reduce.8.cloned.1.call-start = ((), (), s32[]{:S(2)}) async-start(), calls=%async_computation.2 | async-start | bytes 2097152 | tf_op jit(solution)/shard_map/while/body/eval_jaxpr/psum | solution.py:9
  848.2 77.2 %all-reduce.6.cloned.1.call-start = ((), (), s32[]{:S(2)}) async-start(), calls=%async_computation.1 | async-start | bytes 2097152 | tf_op jit(solution)/shard_map/while/body/eval_jaxpr/psum | solution.py:9
  867.3 125.2 %all-reduce.8.cloned.1.call-start = ((), (), s32[]{:S(2)}) async-start(), calls=%async_computation.2 | async-start | bytes 2097152 | tf_op jit(solution)/shard_map/while/body/eval_jaxpr/psum | solution.py:9
  994.1 77.2 %all-reduce.6.cloned.1.call-start = ((), (), s32[]{:S(2)}) async-start(), calls=%async_computation.1 | async-start | bytes 2097152 | tf_op jit(solution)/shard_map/while/body/eval_jaxpr/psum | solution.py:9
  1013.2 125.2 %all-reduce.8.cloned.1.call-start = ((), (), s32[]{:S(2)}) async-start(), calls=%async_computation.2 | async-start | bytes 2097152 | tf_op jit(solution)/shard_map/while/body/eval_jaxpr/psum | solution.py:9
  1140.0 77.2 %all-reduce.6.cloned.1.call-start = ((), (), s32[]{:S(2)}) async-start(), calls=%async_computation.1 | async-start | bytes 2097152 | tf_op jit(solution)/shard_map/while/body/eval_jaxpr/psum | solution.py:9
  1159.1 124.3 %all-reduce.8.cloned.1.call-start = ((), (), s32[]{:S(2)}) async-start(), calls=%async_computation.2 | async-start | bytes 2097152 | tf_op jit(solution)/shard_map/while/body/eval_jaxpr/psum | solution.py:9
  1284.9 1.3 copy-start.1
Sparse Core Ops, SparseCore 0:
  25.3 70.7 all-reduce.3
  136.1 59.0 all-reduce.5
  210.8 50.5 all-reduce.7
  282.1 57.9 all-reduce.5
  348.6 58.6 all-reduce.7
  428.0 57.9 all-reduce.5
  494.4 59.5 all-reduce.7
  574.8 57.9 all-reduce.5
  641.2 59.5 all-reduce.7
  721.6 57.9 all-reduce.5
  788.0 58.6 all-reduce.7
  867.5 57.9 all-reduce.5
  933.9 58.6 all-reduce.7
  1013.3 57.9 all-reduce.5
  1079.8 58.6 all-reduce.7
  1159.2 57.9 all-reduce.5
  1232.9 50.5 all-reduce.7
where the time goes:
time: 1300 us; the launch traced here: 1290 us
  waiting for transfers between devices  922 us (71%)
  other arithmetic  165 us (13%)
  local copies, waits for them, and re-layouts  125 us (10%)
  loops' own time  42.4 us (3%)
  matrix products  23.4 us (2%)
  between operations  13.9 us (1%)
    psum x16, waiting for transfers between devices, broadcast(): return lax.psum(block, axis)  922 us
    select_n x16, other arithmetic, broadcast(): jnp.where(lax.axis_index(axis) == source, block, jnp.zeros_like(block))  114 us
    gather x2, local copies, waits for them, and re-layouts, per_device(): jnp.diagonal(gram[:, slot * blk_width:(slot + 1) * blk_width])  65 us
    another operation x1, loops' own time, per_device(): beta, grad = lax.fori_loop(0, order.shape[0], visit, (beta, grad))  42.4 us
    dynamic_update_slice x8, other arithmetic, visit(): lax.dynamic_update_index_in_dim(beta, beta_old + arrived.astype(jnp.float...  32.3 us
  transfers between devices with their start and end apart: 17, of which 16 were waited for; matrix products, arithmetic and copies ran while one was open for 7% of the time, Pallas kernels for 0%

commit v1 on v0

v1 whole, which is shorter than its diff:
```python
import functools

import jax
import jax.numpy as jnp
import numpy as np
from jax import lax
from jax.experimental import pallas as pl
from jax.experimental.pallas import tpu as pltpu
from jax.sharding import PartitionSpec as P

NT = (((1,), (1,)), ((), ()))


def device_pairs(flows, planes, lines):
    nxt = dict(flows)
    for start in [a for a in nxt if a not in nxt.values()]:
        end = start
        while end in nxt:
            end = nxt[end]
        nxt[end] = start
    pairs = []
    for z in range(planes):
        for q in range(lines):
            for k in range(2):
                to_z, to_q = nxt.get((z, q), (z, q))
                to_k = k if (z, q) in nxt else 1 - k
                pairs.append(((2 * z + k) * lines + q, (2 * to_z + to_k) * lines + to_q))
    return pairs


def step_kernel(s_ref, lam_ref, act_ref, pen_ref, diag_ref, beta_ref, grad_ref, acc_ref, next_ref, *rest):
    *got, step_ref, pay_ref = rest
    beta_old, diag = beta_ref[0], diag_ref[0]
    grad = grad_ref[0] - acc_ref[0]
    for r in got:
        grad = grad - r[...].astype(jnp.float32)
    shifted = diag * beta_old + grad
    size = jnp.maximum(jnp.abs(shifted) - lam_ref[...] * pen_ref[0], 0.0) / diag
    beta_new = jnp.where(shifted < 0.0, -size, size)
    step = jnp.where(act_ref[0] == 1, beta_new - beta_old, 0.0).astype(jnp.bfloat16)
    step_ref[...] = step

    @pl.when(s_ref[3] == 1)
    def _():
        pay_ref[...] = step

    @pl.when(s_ref[3] == 0)
    def _():
        pay_ref[...] = next_ref[0].astype(pay_ref.dtype)


def soft_step(scalars, lam, act, pen, diag, beta, grad, acc, got, tile=512):
    _, resp, width = beta.shape
    column = pl.BlockSpec((resp, 1), lambda i, s: (0, 0))
    line = pl.BlockSpec((1, 1, tile), lambda i, s: (s[0], 0, i))
    now = pl.BlockSpec((1, resp, tile), lambda i, s: (s[0], 0, i))
    after = pl.BlockSpec((1, resp, tile), lambda i, s: (s[2], 0, i))
    flat = pl.BlockSpec((resp, tile), lambda i, s: (0, i))
    return pl.pallas_call(
        step_kernel,
        grid_spec=pltpu.PrefetchScalarGridSpec(
            num_scalar_prefetch=1,
            grid=(width // tile,),
            in_specs=[column, pl.BlockSpec((1, resp, 1), lambda i, s: (s[1], 0, 0)), line, line, now, now, now, after]
            + [flat] * len(got),
            out_specs=[flat, flat],
        ),
        out_shape=[jax.ShapeDtypeStruct((resp, width), jnp.bfloat16)] * 2,
        compiler_params=pltpu.CompilerParams(dimension_semantics=("arbitrary",)),
        cost_estimate=pl.CostEstimate(flops=20 * resp * width, bytes_accessed=22 * resp * width, transcendentals=0),
    )(scalars, lam, act, pen, diag, beta, grad, acc, acc, *got)


def times_block(x, own, own_ref, sib_ref):
    block = jnp.where(own == 1, own_ref[...], sib_ref[...])
    change = lax.dot_general(x, block, NT, preferred_element_type=jnp.float32)
    return change.astype(jnp.bfloat16).astype(jnp.float32)


def relay_kernel(s_ref, x_ref, step_ref, own_ref, sib_ref, acc_ref, send_ref, *, tile):
    i = pl.program_id(0)

    @pl.when(s_ref[0] == 1)
    def _():
        total = acc_ref[0] + times_block(x_ref[...], s_ref[2], own_ref, sib_ref)
        send_ref[...] = total.astype(send_ref.dtype)

    @pl.when(s_ref[0] == 0)
    def _():
        send_ref[...] = step_ref[...]


def relay(scalars, x, step, g_own, g_sib, acc, tile=512):
    resp, width = x.shape
    flat = pl.BlockSpec((resp, tile), lambda i, s: (0, i))
    return pl.pallas_call(
        functools.partial(relay_kernel, tile=tile),
        grid_spec=pltpu.PrefetchScalarGridSpec(
            num_scalar_prefetch=1,
            grid=(width // tile,),
            in_specs=[
                pl.BlockSpec((resp, width), lambda i, s: (0, 0)),
                flat,
                pl.BlockSpec((tile, width), lambda i, s: (i * s[0] * s[2], s[3])),
                pl.BlockSpec((tile, width), lambda i, s: (i * s[0] * (1 - s[2]), s[3])),
                pl.BlockSpec((1, resp, tile), lambda i, s: (s[1], 0, i)),
            ],
            out_specs=flat,
        ),
        out_shape=jax.ShapeDtypeStruct((resp, width), jnp.bfloat16),
        compiler_params=pltpu.CompilerParams(dimension_semantics=("arbitrary",), vmem_limit_bytes=32 << 20),
        cost_estimate=pl.CostEstimate(
            flops=2 * resp * width * width, bytes_accessed=2 * width * width, transcendentals=0
        ),
    )(scalars, x, step, g_own, g_sib, acc)


def update_kernel(s_ref, own_ref, sib_ref, acc_ref, moved_ref, *rest):
    *arrived, out_ref, moved_out, x_ref = rest
    j, i = pl.program_id(0), pl.program_id(1)
    live, own = s_ref[0], 1 - (s_ref[1] ^ j)

    @pl.when((i == 0) & (j == 0))
    def _():
        for n, r in enumerate(arrived):
            @pl.when(s_ref[3] == n)
            def _():
                x_ref[...] = r[...]

        @pl.when(live == 1)
        def _():
            moved_out[0] = x_ref[...]

        @pl.when(live == 0)
        def _():
            moved_out[0] = moved_ref[0]

    @pl.when(live == 1)
    def _():
        out_ref[0] = acc_ref[0] + times_block(x_ref[...], own, own_ref, sib_ref)

    @pl.when(live == 0)
    def _():
        out_ref[0] = acc_ref[0]


def update(scalars, g_own, g_sib, acc, moved, arrived, tile=512):
    _, resp, width = acc.shape
    acc_spec = pl.BlockSpec((1, resp, tile), lambda j, i, s: (j, 0, i))
    moved_spec = pl.BlockSpec((1, resp, width), lambda j, i, s: (s[2], 0, 0))
    full = pl.BlockSpec((resp, width), lambda j, i, s: (0, 0))
    return pl.pallas_call(
        update_kernel,
        grid_spec=pltpu.PrefetchScalarGridSpec(
            num_scalar_prefetch=1,
            grid=(2, width // tile),
            in_specs=[
                pl.BlockSpec((tile, width), lambda j, i, s: (i * s[0] * (1 - (s[1] ^ j)), s[2])),
                pl.BlockSpec((tile, width), lambda j, i, s: (i * s[0] * (s[1] ^ j), s[2])),
                acc_spec,
                moved_spec,
            ] + [full] * len(arrived),
            out_specs=[acc_spec, moved_spec],
            scratch_shapes=[pltpu.VMEM((resp, width), jnp.bfloat16)],
        ),
        out_shape=[jax.ShapeDtypeStruct(acc.shape, acc.dtype), jax.ShapeDtypeStruct(moved.shape, moved.dtype)],
        input_output_aliases={3: 0, 4: 1},
        compiler_params=pltpu.CompilerParams(
            dimension_semantics=("arbitrary", "arbitrary"), vmem_limit_bytes=40 << 20
        ),
        cost_estimate=pl.CostEstimate(
            flops=4 * resp * width * width, bytes_accessed=4 * width * width, transcendentals=0
        ),
    )(scalars, g_own, g_sib, acc, moved, *arrived)


def per_device(planes, lines, gram, corr, beta_start, lambdas, penalty, strong, active, order):
    width = corr.shape[0]
    lam_count, phenos = beta_start.shape[1:]
    cols = lam_count * phenos
    half = cols // 2
    row = lax.axis_index("row")
    z, k, q = row // 2, row % 2, lax.axis_index("col")
    swap = [(r * lines + c, (r ^ 1) * lines + c) for r in range(2 * planes) for c in range(lines)]
    permute = lambda x, pairs: lax.ppermute(x, ("row", "col"), pairs)
    ordered = lambda mine, other: jnp.where(k == 0, jnp.stack([mine, other]), jnp.stack([other, mine]))

    def gather_col(x):
        return lax.all_to_all(jnp.broadcast_to(x[None], (lines, *x.shape)), "col", 0, 0)

    g_sib = permute(gram, swap)

    fine = 128
    wanted = penalty.reshape(-1, fine)[strong // fine]
    pen_own = jnp.sum(jnp.where(lax.broadcasted_iota(jnp.int32, wanted.shape, 1) == (strong % fine)[:, None], wanted, 0.0), axis=1)
    tiles = width // fine
    slot = lax.dynamic_slice_in_dim(gram, k * width, width, 1)
    square = jnp.stack([slot[i * fine : (i + 1) * fine, i * fine : (i + 1) * fine] for i in range(tiles)])
    diag_own = jnp.sum(jnp.where(jnp.eye(fine, dtype=bool)[None], square.astype(jnp.float32), 0.0), axis=1).reshape(width)
    small_own = jnp.stack([pen_own, diag_own])
    small = ordered(small_own, permute(small_own, swap))
    pen, diag = small[:, :1], small[:, 1:]

    flat = beta_start.reshape(2 * width, cols)
    product = jnp.dot(gram, flat.astype(jnp.bfloat16), preferred_element_type=jnp.float32).T
    shares = lax.all_to_all(product.reshape(lines, cols // lines, width), "col", 0, 0)
    summed = gather_col(jnp.sum(shares, axis=0)).reshape(cols, width)
    grad_own = jnp.tile(corr.T, (lam_count, 1)) - summed
    grad_half = grad_own.reshape(2, half, width)
    mine = lax.dynamic_index_in_dim(grad_half, k, 0, keepdims=False)
    other = permute(lax.dynamic_index_in_dim(grad_half, 1 - k, 0, keepdims=False), swap)
    grad0 = ordered(mine, other)

    beta_half = lax.dynamic_slice_in_dim(flat, k * half, half, 1).reshape(2, width, half)
    beta0 = jnp.swapaxes(beta_half, 1, 2)
    lam = lax.dynamic_slice_in_dim(jnp.repeat(lambdas, phenos), k * half, half)[:, None]
    act = lax.dynamic_slice_in_dim(jnp.repeat(active.T, phenos, axis=1), k * half, half, 1)[:, :, None]
    flag = lambda v: v.astype(jnp.int32)

    def routes(p, pn):
        rest_q = [c for c in range(lines) if c not in (p, pn)]
        rest_z = sorted([c for c in range(planes) if c not in (p, pn)], key=lambda c: abs(c - p) - abs(c - pn))
        if p == pn:
            return [([((p, p), (c, p)), ((p, c), (p, p))], c, p) for c in rest_z]
        first = ([((p, p), (pn, p))] + [((pn, c), (pn, pn)) for c in rest_q[:1]], pn, p)
        last = ([((pn, p), (pn, pn))] + [((p, p), (c, p)) for c in rest_z[:1]], rest_z[0] if rest_z else pn, p)
        between = []
        for line, plane in zip(rest_q[1:], rest_z[1:]):
            source = p if abs(plane - p) <= abs(plane - pn) else pn
            between.append(([((source, p), (plane, p)), ((pn, line), (pn, pn))], plane, source))
        return [first, *between, last]

    holds = np.zeros((planes, planes, planes), np.int32)
    for p in range(planes):
        for pn in range(planes):
            for n, (_, plane, _) in enumerate(routes(p, pn)):
                holds[p, pn, plane] = n + 1
            holds[p, pn, p] = 0

    def branch(p, pn):
        plan = routes(p, pn)
        send = lambda payload, flows: permute(payload, device_pairs(flows, planes, lines))

        def run(operands):
            step, pay, acc, g_own, g_sib, s, sn = operands
            if p == pn:
                return tuple(send(pay, flows) for flows, _, _ in plan)
            at_pn = (z == pn) & (q == p)
            first = send(pay, plan[0][0])
            scalars = jnp.stack([flag(at_pn), sn, flag(k == sn), s])
            out = relay(scalars, first, step, g_own, g_sib, acc)
            between = [
                send(pay if source == p else jnp.where(at_pn, first, pay), flows) for flows, _, source in plan[1:-1]
            ]
            return (first, *between, send(out, plan[-1][0]))

        return run

    branches = [branch(p, pn) for p in range(planes) for pn in range(planes)]
    visits = order.shape[0]

    def visit(turn, carry):
        acc, moved, got = carry
        block = order[turn]
        after = order[jnp.minimum(turn + 1, visits - 1)]
        p, s, pn, sn = block // 2, block % 2, after // 2, after % 2
        live = flag(q == p)
        scalars = jnp.stack([s, block, sn, flag((z == p) & (q == p))])
        step, pay = soft_step(scalars, lam, act, pen, diag, beta0, grad0, acc, got)
        got = lax.switch(p * planes + pn, branches, (step, pay, acc, gram, g_sib, s, sn))
        scalars = jnp.stack([live, k, s, jnp.asarray(holds)[p, pn, z]])
        acc, moved = update(scalars, gram, g_sib, acc, moved, (step, *got))
        return acc, moved, got

    zero = jnp.zeros((2, half, width), jnp.float32)
    small_zero = zero.astype(jnp.bfloat16)
    acc, moved, _ = lax.fori_loop(0, visits, visit, (zero, small_zero, (small_zero[0],) * (planes - 1)))

    moved_all = ordered(moved, permute(moved, swap))
    moved_all = moved_all.transpose(1, 3, 0, 2).reshape(2 * width, cols)
    beta = (flat + moved_all.astype(jnp.float32)).reshape(beta_start.shape)

    share = acc.astype(jnp.bfloat16).reshape(2, lines, half // lines, width).swapaxes(0, 1)
    share = jnp.sum(lax.all_to_all(share, "col", 0, 0).astype(jnp.float32), axis=0)
    at = lax.axis_index("col") * (half // lines)
    share = (lax.dynamic_slice_in_dim(grad0, at, half // lines, 1) - share).astype(jnp.bfloat16)
    final = gather_col(share).swapaxes(0, 1).reshape(2, half, width)
    mine = lax.dynamic_index_in_dim(final, k, 0, keepdims=False)
    other = permute(lax.dynamic_index_in_dim(final, 1 - k, 0, keepdims=False), swap)
    final = ordered(mine, other).reshape(cols, width)
    grad = final.T.reshape(width, lam_count, phenos).astype(jnp.float32)
    return beta, grad


def solution(mesh):
    planes, lines = mesh.shape["row"] // 2, mesh.shape["col"]
    in_specs = (P("row", "col"), P("row", None), P("col", None, None), P(), P(), P("row"), P(), P())
    out_specs = (P("col", None, None), P("row", None, None))
    return jax.shard_map(
        functools.partial(per_device, planes, lines),
        mesh=mesh, in_specs=in_specs, out_specs=out_specs, check_vma=False,
    )
```

time: 1300 us -> 652 us (0.50)
  waiting for transfers between devices: 922 us -> 105 us
  starting transfers between devices: 0.71 us -> 264 us
  other arithmetic: 165 us -> 33.7 us
  Pallas kernels: 0 us -> 111 us
  local copies, waits for them, and re-layouts: 125 us -> 78.3 us
    psum x17 -> x0, waiting for transfers between devices: 922 us -> none  [the longest x16 922 us: broadcast(): return lax.psum(block, axis)]
    ppermute x0 -> x29, starting transfers between devices: none -> 220 us  [per_device(): permute = lambda x, pairs: lax.ppermute(x, ('row', 'col'), pairs)]
    select_n x24 -> x9, other arithmetic: 114 us -> 2.23 us  [the longest x3 1.76 us: per_device(): jnp.where(k == 0, jnp.stack([mine, other]), jnp.stack([other, mine]))]
    pallas_call x0 -> x22, Pallas kernels: none -> 111 us  [the longest x8 59.9 us: update(): pl.pallas_call(update_kernel, grid_spec=pltpu.PrefetchScalarGridSpec(num_...]
    ppermute x0 -> x29, waiting for transfers between devices: none -> 70.8 us  [per_device(): permute = lambda x, pairs: lax.ppermute(x, ('row', 'col'), pairs)]
    gather x3 -> x1, local copies, waits for them, and re-layouts: 76.8 us -> 7.64 us  [per_device(): wanted = penalty.reshape(-1, fine)[strong // fine]]
    all_to_all x0 -> x4, starting transfers between devices: none -> 44.7 us  [the longest x1 33.6 us: per_device(): lax.all_to_all(share, 'col', 0, 0).astype(jnp.float32)]
    all_to_all x0 -> x4, waiting for transfers between devices: none -> 34.5 us  [the longest x1 14.6 us: per_device(): lax.all_to_all(share, 'col', 0, 0).astype(jnp.float32)]
  transfers between devices with their start and end apart: 17 -> 33, of which waited for: 16 -> 22; matrix products, arithmetic and copies ran while one was open for 7% -> 12% of each run, Pallas kernels for 0% -> 1%
where the time goes in v1:
time: 652 us; the launch traced here: 651 us
  starting transfers between devices  264 us (40%)
  Pallas kernels  111 us (17%)
  waiting for transfers between devices  105 us (16%)
  local copies, waits for them, and re-layouts  78.3 us (12%)
  loops' own time  44.7 us (7%)
  other arithmetic  33.7 us (5%)
  matrix products  12.2 us (2%)
    ppermute x29, starting transfers between devices, per_device(): permute = lambda x, pairs: lax.ppermute(x, ('row', 'col'), pairs)  220 us
    ppermute x29, waiting for transfers between devices, per_device(): permute = lambda x, pairs: lax.ppermute(x, ('row', 'col'), pairs)  70.8 us
    pallas_call x8, Pallas kernels, update(): pl.pallas_call(update_kernel, grid_spec=pltpu.PrefetchScalarGridSpec(num_...  59.9 us
    another operation x1, loops' own time, per_device(): lax.fori_loop(0, visits, visit, (zero, small_zero, (small_zero[0],) * (pl...  44.2 us
    all_to_all x1, starting transfers between devices, per_device(): lax.all_to_all(share, 'col', 0, 0).astype(jnp.float32)  33.6 us
    pallas_call x8, Pallas kernels, soft_step(): pl.pallas_call(step_kernel, grid_spec=pltpu.PrefetchScalarGridSpec(num_sc...  31.7 us
    unnamed x42, local copies, waits for them, and re-layouts  27.3 us
    pallas_call x6, Pallas kernels, relay(): pl.pallas_call(functools.partial(relay_kernel, tile=tile), grid_spec=pltp...  19.7 us
  transfers between devices with their start and end apart: 33, of which 22 were waited for; matrix products, arithmetic and copies ran while one was open for 12% of the time, Pallas kernels for 1%

profile of v1, /device:TPU:8, one launch (start us, length us, event | category | flops | bytes accessed | tf_op | source)
XLA Modules:
  0.0 650.8 jit_solution(9346046484973317404)
XLA Ops:
  6.2 12.2 %fusion = f32[4,64,2048]{2,1,0:T(8,128)} fusion(bf16[4,64,4096]{2,1,0:T(8,128)(2,1)} %bitcast.208, bf16[2048,4096]{1,0:T(8,128)(2,1)} %param.27), kind=kOutput, calls=%fused_computation.23 | convolution fusion | flops 4294967296 | bytes 20971520 | tf_op jit(solution)/shard_map/dot_general | solution.py:205
  22.3 7.6 %gather_fusion = f32[2048,128]{1,0:T(8,128)} fusion(f32[2048,128]{1,0:T(8,128)S(1)} %bitcast.197, s32[2048]{0:T(1024)S(1)} %get-tuple-element.1102), kind=kCustom, calls=%fused_computation | custom fusion | bytes 2105344 | tf_op jit(solution)/shard_map/gather | solution.py:194
  41.5 6.4 all-to-all-done
  67.3 10.8 %all-to-all-done.1 = f32[4,64,2048]{2,1,0:T(8,128)S(1)} async-done(((f32[4,64,2048]{2,1,0:T(8,128)}), f32[4,64,2048]{2,1,0:T(8,128)S(1)}, u32[]{:S(2)}, u32[]{:S(2)}) %all-to-all-start.1) | async-done | bytes 2097184 | tf_op jit(solution)/shard_map/all_to_all | solution.py:189
  92.4 478.4 %while.25 = (s32[]{:T(128)}, f32[2,128,2048]{2,1,0:T(8,128)S(1)}, bf16[2,128,2048]{2,1,0:T(8,128)(2,1)}, bf16[128,2048]{1,0:T(8,128)(2,1)}, bf16[128,2048]{1,0:T...) while((s32[]{:T(128)}, f32[2,128,2048]{2,1,0:T(8,128)S(1)}, ...), condition=%wide.region_20.21_spmd.clone, body=%wide.region_3.20_spmd.sunk.clone.sunk | while | flops 3226730496 | bytes 38798516 | solution.py:277
  105.8 8.4 %conditional.4 = (bf16[128,2048]{1,0:T(8,128)(2,1)}, bf16[128,2048]{1,0:T(8,128)(2,1)}, bf16[128,2048]{1,0:T(8,128)(2,1)}) conditional(s32[]{:T(128)} %clamp.16, bf16[128,2048]{1,0:T(8,128)(2,1)S(1)} %get-tuple-element.1234, (bf16[128,2048]{1,0:T(8,128)(2,1)S(1)}, s32[]{:T(128)}, s32[]{:T(128)}, s32[]{:T(128)}, ...), branch_computations={%region_4.4_spmd, %region_5.5_spmd, %region_6.6_spmd, %region_7.7_... | conditional | flops 1074003968 | bytes 16253145 | solution.py:270
  133.0 77.7 %conditional.4 = (bf16[128,2048]{1,0:T(8,128)(2,1)}, bf16[128,2048]{1,0:T(8,128)(2,1)}, bf16[128,2048]{1,0:T(8,128)(2,1)}) conditional(s32[]{:T(128)} %clamp.16, bf16[128,2048]{1,0:T(8,128)(2,1)S(1)} %get-tuple-element.1234, (bf16[128,2048]{1,0:T(8,128)(2,1)S(1)}, s32[]{:T(128)}, s32[]{:T(128)}, s32[]{:T(128)}, ...), branch_computations={%region_4.4_spmd, %region_5.5_spmd, %region_6.6_spmd, %region_7.7_... | conditional | flops 1074003968 | bytes 16253145 | solution.py:270
  133.0 41.0 %collective-permute-start.18 = (bf16[128,2048]{1,0:T(8,128)(2,1)S(1)}, bf16[128,2048]{1,0:T(8,128)(2,1)}, u32[]{:S(2)}, u32[]{:S(2)}) collective-permute-start(bf16[128,2048]{1,0:T(8,128)(2,1)S(1)} %get-tuple-element.748), channel_id=1, source_target_pairs={{0,24},{4,28},{1,5},{5,1},{2,6},{6,2},{3,7},{7,3},{8,12},{12,8},{9... | collective-permute-start | bytes 1572872 | tf_op jit(solution)/shard_map/while/body/eval_jaxpr/cond/branch_3_fun/ppermute | solution.py:185
  179.0 19.0 %collective-permute-start.20 = (bf16[128,2048]{1,0:T(8,128)(2,1)S(1)}, bf16[128,2048]{1,0:T(8,128)(2,1)}, u32[]{:S(2)}, u32[]{:S(2)}) collective-permute-start(bf16[128,2048]{1,0:T(8,128)(2,1)S(1)} %branch_3_fun.1), channel_id=1, source_target_pairs={{0,8},{4,12},{1,5},{5,1},{2,6},{6,2},{3,7},{7,3},{8,0},{12,4},{9,1... | collective-permute-start | bytes 1572872 | tf_op jit(solution)/shard_map/while/body/eval_jaxpr/cond/branch_3_fun/ppermute | solution.py:185
  198.3 12.4 %collective-permute-done.20 = bf16[128,2048]{1,0:T(8,128)(2,1)} collective-permute-done((bf16[128,2048]{1,0:T(8,128)(2,1)S(1)}, bf16[128,2048]{1,0:T(8,128)(2,1)}, u32[]{:S(2)}, u32[]{:S(2)}) %collective-permute-start.20) | collective-permute-done | bytes 524320 | tf_op jit(solution)/shard_map/while/body/eval_jaxpr/cond/branch_3_fun/ppermute | solution.py:185
  210.7 13.9 %eval_jaxpr.19 = (f32[2,128,2048]{2,1,0:T(8,128)S(1)}, bf16[2,128,2048]{2,1,0:T(8,128)(2,1)}) custom-call(s32[4]{0:T(128)S(1)} %get-tuple-element.1231.s_ref, bf16[2048,4096]{1,0:T(8,128)(2,1)} %get-tuple-element.1361.own_ref, bf16[2048,4096]{1,0:T(8,128)(2,1)} %get-tuple-element.1362.sib_ref, ...), custom_call_target="tpu_custom_call", output_to_operand_aliasing={{0}: (3, {}), {1}: (4, {})} | custom-call | flops 2147483648 | bytes 16777216 | tf_op jit(solution)/shard_map/while/body/eval_jaxpr/pallas_call | solution.py:152
  238.1 29.8 %conditional.4 = (bf16[128,2048]{1,0:T(8,128)(2,1)}, bf16[128,2048]{1,0:T(8,128)(2,1)}, bf16[128,2048]{1,0:T(8,128)(2,1)}) conditional(s32[]{:T(128)} %clamp.16, bf16[128,2048]{1,0:T(8,128)(2,1)S(1)} %get-tuple-element.1234, (bf16[128,2048]{1,0:T(8,128)(2,1)S(1)}, s32[]{:T(128)}, s32[]{:T(128)}, s32[]{:T(128)}, ...), branch_computations={%region_4.4_spmd, %region_5.5_spmd, %region_6.6_spmd, %region_7.7_... | conditional | flops 1074003968 | bytes 16253145 | solution.py:270
  243.5 21.9 %collective-permute-start.47 = (bf16[128,2048]{1,0:T(8,128)(2,1)S(1)}, bf16[128,2048]{1,0:T(8,128)(2,1)}, u32[]{:S(2)}, u32[]{:S(2)}) collective-permute-start(bf16[128,2048]{1,0:T(8,128)(2,1)S(1)} %branch_14_fun.1), channel_id=1, source_target_pairs={{0,4},{4,0},{1,5},{5,1},{2,6},{6,2},{3,27},{7,31},{8,12},{12,8},{9... | collective-permute-start | bytes 1572872 | tf_op jit(solution)/shard_map/while/body/eval_jaxpr/cond/branch_14_fun/ppermute | solution.py:185
  286.6 47.6 %conditional.4 = (bf16[128,2048]{1,0:T(8,128)(2,1)}, bf16[128,2048]{1,0:T(8,128)(2,1)}, bf16[128,2048]{1,0:T(8,128)(2,1)}) conditional(s32[]{:T(128)} %clamp.16, bf16[128,2048]{1,0:T(8,128)(2,1)S(1)} %get-tuple-element.1234, (bf16[128,2048]{1,0:T(8,128)(2,1)S(1)}, s32[]{:T(128)}, s32[]{:T(128)}, s32[]{:T(128)}, ...), branch_computations={%region_4.4_spmd, %region_5.5_spmd, %region_6.6_spmd, %region_7.7_... | conditional | flops 1074003968 | bytes 16253145 | solution.py:270
  288.2 12.7 %collective-permute-done.33.x_ref = bf16[128,2048]{1,0:T(8,128)(2,1)} collective-permute-done((bf16[128,2048]{1,0:T(8,128)(2,1)S(1)}, bf16[128,2048]{1,0:T(8,128)(2,1)}, u32[]{:S(2)}, u32[]{:S(2)}) %collective-permute-start.33) | collective-permute-done | bytes 524320 | tf_op jit(solution)/shard_map/while/body/eval_jaxpr/cond/branch_9_fun/ppermute | solution.py:185
  304.4 28.1 %collective-permute-start.34 = (bf16[128,2048]{1,0:T(8,128)(2,1)S(1)}, bf16[128,2048]{1,0:T(8,128)(2,1)}, u32[]{:S(2)}, u32[]{:S(2)}) collective-permute-start(bf16[128,2048]{1,0:T(8,128)(2,1)S(1)} %broadcast_select_fusion.4), channel_id=1, source_target_pairs={{0,4},{4,0},{1,5},{5,1},{2,10},{6,14},{3,7},{7,3},{8,12},{12,8},{9... | collective-permute-start | bytes 1572872 | tf_op jit(solution)/shard_map/while/body/eval_jaxpr/cond/branch_9_fun/ppermute | solution.py:185
  352.9 37.9 %conditional.4 = (bf16[128,2048]{1,0:T(8,128)(2,1)}, bf16[128,2048]{1,0:T(8,128)(2,1)}, bf16[128,2048]{1,0:T(8,128)(2,1)}) conditional(s32[]{:T(128)} %clamp.16, bf16[128,2048]{1,0:T(8,128)(2,1)S(1)} %get-tuple-element.1234, (bf16[128,2048]{1,0:T(8,128)(2,1)S(1)}, s32[]{:T(128)}, s32[]{:T(128)}, s32[]{:T(128)}, ...), branch_computations={%region_4.4_spmd, %region_5.5_spmd, %region_6.6_spmd, %region_7.7_... | conditional | flops 1074003968 | bytes 16253145 | solution.py:270
  353.0 22.8 %collective-permute-start.3 = (bf16[128,2048]{1,0:T(8,128)(2,1)S(1)}, bf16[128,2048]{1,0:T(8,128)(2,1)}, u32[]{:S(2)}, u32[]{:S(2)}) collective-permute-start(bf16[128,2048]{1,0:T(8,128)(2,1)S(1)} %param.5), channel_id=1, source_target_pairs={{0,4},{4,0},{1,8},{5,12},{2,6},{6,2},{3,7},{7,3},{8,9},{12,13},{9,... | collective-permute-start | bytes 1572872 | tf_op jit(solution)/shard_map/while/body/eval_jaxpr/cond/branch_5_fun/ppermute | solution.py:185
  376.3 14.5 %collective-permute-done.3 = bf16[128,2048]{1,0:T(8,128)(2,1)} collective-permute-done((bf16[128,2048]{1,0:T(8,128)(2,1)S(1)}, bf16[128,2048]{1,0:T(8,128)(2,1)}, u32[]{:S(2)}, u32[]{:S(2)}) %collective-permute-start.3) | collective-permute-done | bytes 524320 | tf_op jit(solution)/shard_map/while/body/eval_jaxpr/cond/branch_5_fun/ppermute | solution.py:185
  409.6 7.5 %conditional.4 = (bf16[128,2048]{1,0:T(8,128)(2,1)}, bf16[128,2048]{1,0:T(8,128)(2,1)}, bf16[128,2048]{1,0:T(8,128)(2,1)}) conditional(s32[]{:T(128)} %clamp.16, bf16[128,2048]{1,0:T(8,128)(2,1)S(1)} %get-tuple-element.1234, (bf16[128,2048]{1,0:T(8,128)(2,1)S(1)}, s32[]{:T(128)}, s32[]{:T(128)}, s32[]{:T(128)}, ...), branch_computations={%region_4.4_spmd, %region_5.5_spmd, %region_6.6_spmd, %region_7.7_... | conditional | flops 1074003968 | bytes 16253145 | solution.py:270
  417.1 5.4 eval_jaxpr.19
  435.9 93.4 %conditional.4 = (bf16[128,2048]{1,0:T(8,128)(2,1)}, bf16[128,2048]{1,0:T(8,128)(2,1)}, bf16[128,2048]{1,0:T(8,128)(2,1)}) conditional(s32[]{:T(128)} %clamp.16, bf16[128,2048]{1,0:T(8,128)(2,1)S(1)} %get-tuple-element.1234, (bf16[128,2048]{1,0:T(8,128)(2,1)S(1)}, s32[]{:T(128)}, s32[]{:T(128)}, s32[]{:T(128)}, ...), branch_computations={%region_4.4_spmd, %region_5.5_spmd, %region_6.6_spmd, %region_7.7_... | conditional | flops 1074003968 | bytes 16253145 | solution.py:270
  435.9 57.6 %collective-permute-start.15 = (bf16[128,2048]{1,0:T(8,128)(2,1)S(1)}, bf16[128,2048]{1,0:T(8,128)(2,1)}, u32[]{:S(2)}, u32[]{:S(2)}) collective-permute-start(bf16[128,2048]{1,0:T(8,128)(2,1)S(1)} %get-tuple-element.738), channel_id=1, source_target_pairs={{0,16},{4,20},{1,5},{5,1},{2,6},{6,2},{3,7},{7,3},{8,12},{12,8},{9... | collective-permute-start | bytes 1572872 | tf_op jit(solution)/shard_map/while/body/eval_jaxpr/cond/branch_2_fun/ppermute | solution.py:185
  498.5 18.1 %collective-permute-start.17 = (bf16[128,2048]{1,0:T(8,128)(2,1)S(1)}, bf16[128,2048]{1,0:T(8,128)(2,1)}, u32[]{:S(2)}, u32[]{:S(2)}) collective-permute-start(bf16[128,2048]{1,0:T(8,128)(2,1)S(1)} %branch_2_fun.1), channel_id=1, source_target_pairs={{0,8},{4,12},{1,5},{5,1},{2,6},{6,2},{3,7},{7,3},{8,0},{12,4},{9,1... | collective-permute-start | bytes 1572872 | tf_op jit(solution)/shard_map/while/body/eval_jaxpr/cond/branch_2_fun/ppermute | solution.py:185
  516.9 12.4 %collective-permute-done.17 = bf16[128,2048]{1,0:T(8,128)(2,1)} collective-permute-done((bf16[128,2048]{1,0:T(8,128)(2,1)S(1)}, bf16[128,2048]{1,0:T(8,128)(2,1)}, u32[]{:S(2)}, u32[]{:S(2)}) %collective-permute-start.17) | collective-permute-done | bytes 524320 | tf_op jit(solution)/shard_map/while/body/eval_jaxpr/cond/branch_2_fun/ppermute | solution.py:185
  529.3 14.0 %eval_jaxpr.19 = (f32[2,128,2048]{2,1,0:T(8,128)S(1)}, bf16[2,128,2048]{2,1,0:T(8,128)(2,1)}) custom-call(s32[4]{0:T(128)S(1)} %get-tuple-element.1231.s_ref, bf16[2048,4096]{1,0:T(8,128)(2,1)} %get-tuple-element.1361.own_ref, bf16[2048,4096]{1,0:T(8,128)(2,1)} %get-tuple-element.1362.sib_ref, ...), custom_call_target="tpu_custom_call", output_to_operand_aliasing={{0}: (3, {}), {1}: (4, {})} | custom-call | flops 2147483648 | bytes 16777216 | tf_op jit(solution)/shard_map/while/body/eval_jaxpr/pallas_call | solution.py:152
  556.6 8.8 %conditional.4 = (bf16[128,2048]{1,0:T(8,128)(2,1)}, bf16[128,2048]{1,0:T(8,128)(2,1)}, bf16[128,2048]{1,0:T(8,128)(2,1)}) conditional(s32[]{:T(128)} %clamp.16, bf16[128,2048]{1,0:T(8,128)(2,1)S(1)} %get-tuple-element.1234, (bf16[128,2048]{1,0:T(8,128)(2,1)S(1)}, s32[]{:T(128)}, s32[]{:T(128)}, s32[]{:T(128)}, ...), branch_computations={%region_4.4_spmd, %region_5.5_spmd, %region_6.6_spmd, %region_7.7_... | conditional | flops 1074003968 | bytes 16253145 | solution.py:270
  556.7 5.6 collective-permute-start.6
  572.0 33.6 %all-to-all-start.2 = ((bf16[4,2,32,2048]{3,2,1,0:T(8,128)(2,1)}), bf16[4,2,32,2048]{3,2,1,0:T(8,128)(2,1)S(1)}, u32[]{:S(2)}, u32[]{:S(2)}) async-start(bf16[4,2,32,2048]{3,2,1,0:T(8,128)(2,1)} %copy.45), calls=%async_computation.2 | async-start | bytes 2097152 | tf_op jit(solution)/shard_map/all_to_all | solution.py:284
  605.6 14.6 %all-to-all-done.2 = bf16[4,2,32,2048]{3,2,1,0:T(8,128)(2,1)S(1)} async-done(((bf16[4,2,32,2048]{3,2,1,0:T(8,128)(2,1)}), bf16[4,2,32,2048]{3,2,1,0:T(8,128)(2,1)S(1)}, u32[]{:S(2)}, u32[]{:S(2)}) %all-to-all-start.2) | async-done | bytes 1048608 | tf_op jit(solution)/shard_map/all_to_all | solution.py:284
  630.1 7.2 %copy.44 = f32[2,2048,2,128]{3,2,1,0:T(2,128)} copy(f32[2,2048,2,128]{1,3,0,2:T(8,128)} %convert_bitcast_fusion) | data formatting | bytes 8388608 | tf_op jit(solution)/shard_map/convert_element_type | solution.py:281
  642.2 5.8 bitcast_add_fusion
  (182 shorter events, 207.5 us)
Async XLA Ops:
  0.6 87.8 %collective-permute-start.50 = (bf16[2048,4096]{1,0:T(8,128)(2,1)}, bf16[2048,4096]{1,0:T(8,128)(2,1)}, u32[]{:S(2)}, u32[]{:S(2)}) collective-permute-start(bf16[2048,4096]{1,0:T(8,128)(2,1)} %param.27), channel_id=1, source_target_pairs={{0,4},{1,5},{2,6},{3,7},{4,0},{5,1},{6,2},{7,3},{8,12},{9,13},{10,... | collective-permute-start | bytes 50331656 | tf_op jit(solution)/shard_map/ppermute | solution.py:185
  18.5 29.4 %all-to-all-start = ((f32[4,64,2048]{2,1,0:T(8,128)}), f32[4,64,2048]{2,1,0:T(8,128)S(1)}, u32[]{:S(2)}, u32[]{:S(2)}) async-start(f32[4,64,2048]{2,1,0:T(8,128)} %fusion), calls=%async_computation | async-start | bytes 4194304 | tf_op jit(solution)/shard_map/all_to_all | solution.py:206
  49.6 28.5 %all-to-all-start.1 = ((f32[4,64,2048]{2,1,0:T(8,128)}), f32[4,64,2048]{2,1,0:T(8,128)S(1)}, u32[]{:S(2)}, u32[]{:S(2)}) async-start(f32[4,64,2048]{2,1,0:T(8,128)} %broadcast_in_dim.60), calls=%async_computation.1 | async-start | bytes 4194304 | tf_op jit(solution)/shard_map/all_to_all | solution.py:189
  58.0 28.8 %collective-permute-start.48 = (f32[2,2048]{1,0:T(2,128)S(1)}, f32[2,2048]{1,0:T(2,128)S(1)}, u32[]{:S(2)}, u32[]{:S(2)}) collective-permute-start(f32[2,2048]{1,0:T(2,128)S(1)} %get-tuple-element.1100), channel_id=1, source_target_pairs={{0,4},{1,5},{2,6},{3,7},{4,0},{5,1},{6,2},{7,3},{8,12},{9,13},{10,... | collective-permute-start | bytes 49160 | tf_op jit(solution)/shard_map/ppermute | solution.py:185
  82.6 4.3 collective-permute-start.49
  105.8 2.2 collective-permute-start.39
  111.4 2.1 collective-permute-start.41
  111.9 2.3 collective-permute-start.40
  133.0 42.7 %collective-permute-start.18 = (bf16[128,2048]{1,0:T(8,128)(2,1)S(1)}, bf16[128,2048]{1,0:T(8,128)(2,1)}, u32[]{:S(2)}, u32[]{:S(2)}) collective-permute-start(bf16[128,2048]{1,0:T(8,128)(2,1)S(1)} %get-tuple-element.748), channel_id=1, source_target_pairs={{0,24},{4,28},{1,5},{5,1},{2,6},{6,2},{3,7},{7,3},{8,12},{12,8},{9... | collective-permute-start | bytes 1572872 | tf_op jit(solution)/shard_map/while/body/eval_jaxpr/cond/branch_3_fun/ppermute | solution.py:185
  179.0 31.7 %collective-permute-start.20 = (bf16[128,2048]{1,0:T(8,128)(2,1)S(1)}, bf16[128,2048]{1,0:T(8,128)(2,1)}, u32[]{:S(2)}, u32[]{:S(2)}) collective-permute-start(bf16[128,2048]{1,0:T(8,128)(2,1)S(1)} %branch_3_fun.1), channel_id=1, source_target_pairs={{0,8},{4,12},{1,5},{5,1},{2,6},{6,2},{3,7},{7,3},{8,0},{12,4},{9,1... | collective-permute-start | bytes 1572872 | tf_op jit(solution)/shard_map/while/body/eval_jaxpr/cond/branch_3_fun/ppermute | solution.py:185
  198.1 12.6 %collective-permute-start.19 = (bf16[128,2048]{1,0:T(8,128)(2,1)S(1)}, bf16[128,2048]{1,0:T(8,128)(2,1)}, u32[]{:S(2)}, u32[]{:S(2)}) collective-permute-start(bf16[128,2048]{1,0:T(8,128)(2,1)S(1)} %broadcast_select_fusion.2), channel_id=1, source_target_pairs={{0,4},{4,0},{1,5},{5,1},{2,6},{6,2},{3,7},{7,3},{8,12},{12,8},{9,1... | collective-permute-start | bytes 1572872 | tf_op jit(solution)/shard_map/while/body/eval_jaxpr/cond/branch_3_fun/ppermute | solution.py:185
  238.1 2.1 collective-permute-start.45
  243.5 23.6 %collective-permute-start.47 = (bf16[128,2048]{1,0:T(8,128)(2,1)S(1)}, bf16[128,2048]{1,0:T(8,128)(2,1)}, u32[]{:S(2)}, u32[]{:S(2)}) collective-permute-start(bf16[128,2048]{1,0:T(8,128)(2,1)S(1)} %branch_14_fun.1), channel_id=1, source_target_pairs={{0,4},{4,0},{1,5},{5,1},{2,6},{6,2},{3,27},{7,31},{8,12},{12,8},{9... | collective-permute-start | bytes 1572872 | tf_op jit(solution)/shard_map/while/body/eval_jaxpr/cond/branch_14_fun/ppermute | solution.py:185
  265.5 2.3 collective-permute-start.46
  286.6 14.4 %collective-permute-start.33 = (bf16[128,2048]{1,0:T(8,128)(2,1)S(1)}, bf16[128,2048]{1,0:T(8,128)(2,1)}, u32[]{:S(2)}, u32[]{:S(2)}) collective-permute-start(bf16[128,2048]{1,0:T(8,128)(2,1)S(1)} %get-tuple-element.798), channel_id=1, source_target_pairs={{0,4},{4,0},{1,5},{5,1},{2,6},{6,2},{3,7},{7,3},{8,9},{12,13},{9,8... | collective-permute-start | bytes 1572872 | tf_op jit(solution)/shard_map/while/body/eval_jaxpr/cond/branch_9_fun/ppermute | solution.py:185
  304.3 28.3 %collective-permute-start.35 = (bf16[128,2048]{1,0:T(8,128)(2,1)S(1)}, bf16[128,2048]{1,0:T(8,128)(2,1)}, u32[]{:S(2)}, u32[]{:S(2)}) collective-permute-start(bf16[128,2048]{1,0:T(8,128)(2,1)S(1)} %branch_9_fun.1), channel_id=1, source_target_pairs={{0,4},{4,0},{1,5},{5,1},{2,6},{6,2},{3,7},{7,3},{8,12},{12,8},{9,1... | collective-permute-start | bytes 1572872 | tf_op jit(solution)/shard_map/while/body/eval_jaxpr/cond/branch_9_fun/ppermute | solution.py:185
  304.4 29.8 %collective-permute-start.34 = (bf16[128,2048]{1,0:T(8,128)(2,1)S(1)}, bf16[128,2048]{1,0:T(8,128)(2,1)}, u32[]{:S(2)}, u32[]{:S(2)}) collective-permute-start(bf16[128,2048]{1,0:T(8,128)(2,1)S(1)} %broadcast_select_fusion.4), channel_id=1, source_target_pairs={{0,4},{4,0},{1,5},{5,1},{2,10},{6,14},{3,7},{7,3},{8,12},{12,8},{9... | collective-permute-start | bytes 1572872 | tf_op jit(solution)/shard_map/while/body/eval_jaxpr/cond/branch_9_fun/ppermute | solution.py:185
  353.0 37.9 %collective-permute-start.3 = (bf16[128,2048]{1,0:T(8,128)(2,1)S(1)}, bf16[128,2048]{1,0:T(8,128)(2,1)}, u32[]{:S(2)}, u32[]{:S(2)}) collective-permute-start(bf16[128,2048]{1,0:T(8,128)(2,1)S(1)} %param.5), channel_id=1, source_target_pairs={{0,4},{4,0},{1,8},{5,12},{2,6},{6,2},{3,7},{7,3},{8,9},{12,13},{9,... | collective-permute-start | bytes 1572872 | tf_op jit(solution)/shard_map/while/body/eval_jaxpr/cond/branch_5_fun/ppermute | solution.py:185
  375.8 15.0 %collective-permute-start.4 = (bf16[128,2048]{1,0:T(8,128)(2,1)S(1)}, bf16[128,2048]{1,0:T(8,128)(2,1)}, u32[]{:S(2)}, u32[]{:S(2)}) collective-permute-start(bf16[128,2048]{1,0:T(8,128)(2,1)S(1)} %param.5), channel_id=1, source_target_pairs={{0,4},{4,0},{1,5},{5,1},{2,6},{6,2},{3,7},{7,3},{8,12},{12,8},{9,1... | collective-permute-start | bytes 1572872 | tf_op jit(solution)/shard_map/while/body/eval_jaxpr/cond/branch_5_fun/ppermute | solution.py:185
  376.0 14.9 %collective-permute-start.5 = (bf16[128,2048]{1,0:T(8,128)(2,1)S(1)}, bf16[128,2048]{1,0:T(8,128)(2,1)}, u32[]{:S(2)}, u32[]{:S(2)}) collective-permute-start(bf16[128,2048]{1,0:T(8,128)(2,1)S(1)} %param.5), channel_id=1, source_target_pairs={{0,4},{4,0},{1,5},{5,1},{2,6},{6,2},{3,7},{7,3},{8,12},{12,8},{9,2... | collective-permute-start | bytes 1572872 | tf_op jit(solution)/shard_map/while/body/eval_jaxpr/cond/branch_5_fun/ppermute | solution.py:185
  409.7 5.5 collective-permute-start.22
  415.0 2.1 collective-permute-start.23
  435.9 59.3 %collective-permute-start.15 = (bf16[128,2048]{1,0:T(8,128)(2,1)S(1)}, bf16[128,2048]{1,0:T(8,128)(2,1)}, u32[]{:S(2)}, u32[]{:S(2)}) collective-permute-start(bf16[128,2048]{1,0:T(8,128)(2,1)S(1)} %get-tuple-element.738), channel_id=1, source_target_pairs={{0,16},{4,20},{1,5},{5,1},{2,6},{6,2},{3,7},{7,3},{8,12},{12,8},{9... | collective-permute-start | bytes 1572872 | tf_op jit(solution)/shard_map/while/body/eval_jaxpr/cond/branch_2_fun/ppermute | solution.py:185
  498.5 30.8 %collective-permute-start.17 = (bf16[128,2048]{1,0:T(8,128)(2,1)S(1)}, bf16[128,2048]{1,0:T(8,128)(2,1)}, u32[]{:S(2)}, u32[]{:S(2)}) collective-permute-start(bf16[128,2048]{1,0:T(8,128)(2,1)S(1)} %branch_2_fun.1), channel_id=1, source_target_pairs={{0,8},{4,12},{1,5},{5,1},{2,6},{6,2},{3,7},{7,3},{8,0},{12,4},{9,1... | collective-permute-start | bytes 1572872 | tf_op jit(solution)/shard_map/while/body/eval_jaxpr/cond/branch_2_fun/ppermute | solution.py:185
  516.6 12.6 %collective-permute-start.16 = (bf16[128,2048]{1,0:T(8,128)(2,1)S(1)}, bf16[128,2048]{1,0:T(8,128)(2,1)}, u32[]{:S(2)}, u32[]{:S(2)}) collective-permute-start(bf16[128,2048]{1,0:T(8,128)(2,1)S(1)} %broadcast_select_fusion.1), channel_id=1, source_target_pairs={{0,4},{4,0},{1,5},{5,1},{2,6},{6,2},{3,7},{7,3},{8,12},{12,8},{9,1... | collective-permute-start | bytes 1572872 | tf_op jit(solution)/shard_map/while/body/eval_jaxpr/cond/branch_2_fun/ppermute | solution.py:185
  556.7 7.3 %collective-permute-start.6 = (bf16[128,2048]{1,0:T(8,128)(2,1)S(1)}, bf16[128,2048]{1,0:T(8,128)(2,1)}, u32[]{:S(2)}, u32[]{:S(2)}) collective-permute-start(bf16[128,2048]{1,0:T(8,128)(2,1)S(1)} %param.10), channel_id=1, source_target_pairs={{0,4},{4,0},{1,5},{5,1},{2,16},{6,20},{3,7},{7,3},{8,12},{12,8},{9... | collective-permute-start | bytes 1572872 | tf_op jit(solution)/shard_map/while/body/eval_jaxpr/cond/branch_10_fun/ppermute | solution.py:185
  562.2 2.4 collective-permute-start.7
  562.4 3.0 collective-permute-start.8
  572.0 48.2 %all-to-all-start.2 = ((bf16[4,2,32,2048]{3,2,1,0:T(8,128)(2,1)}), bf16[4,2,32,2048]{3,2,1,0:T(8,128)(2,1)S(1)}, u32[]{:S(2)}, u32[]{:S(2)}) async-start(bf16[4,2,32,2048]{3,2,1,0:T(8,128)(2,1)} %copy.45), calls=%async_computation.2 | async-start | bytes 2097152 | tf_op jit(solution)/shard_map/all_to_all | solution.py:284
  605.6 20.4 %collective-permute-start.51 = (bf16[2,128,2048]{2,1,0:T(8,128)(2,1)S(1)}, bf16[2,128,2048]{2,1,0:T(8,128)(2,1)}, u32[]{:S(2)}, u32[]{:S(2)}) collective-permute-start(bf16[2,128,2048]{2,1,0:T(8,128)(2,1)S(1)} %copy-done.2), channel_id=1, source_target_pairs={{0,4},{1,5},{2,6},{3,7},{4,0},{5,1},{6,2},{7,3},{8,12},{9,13},{10,... | collective-permute-start | bytes 3145736 | tf_op jit(solution)/shard_map/ppermute | solution.py:185
  622.5 17.5 %all-to-all-start.3 = ((bf16[4,2,32,2048]{3,2,1,0:T(8,128)(2,1)}), bf16[4,2,32,2048]{3,2,1,0:T(8,128)(2,1)S(1)}, u32[]{:S(2)}, u32[]{:S(2)}) async-start(bf16[4,2,32,2048]{3,2,1,0:T(8,128)(2,1)} %broadcast_in_dim.61), calls=%async_computation.3 | async-start | bytes 2097152 | tf_op jit(solution)/shard_map/all_to_all | solution.py:189
  640.2 7.7 %collective-permute-start.52 = (bf16[128,2048]{1,0:T(8,128)(2,1)S(1)}, bf16[128,2048]{1,0:T(8,128)(2,1)S(1)}, u32[]{:S(2)}, u32[]{:S(2)}) collective-permute-start(bf16[128,2048]{1,0:T(8,128)(2,1)S(1)} %get-tuple-element.1096), channel_id=1, source_target_pairs={{0,4},{1,5},{2,6},{3,7},{4,0},{5,1},{6,2},{7,3},{8,12},{9,13},{10,... | collective-permute-start | bytes 1572872 | tf_op jit(solution)/shard_map/ppermute | solution.py:185
  (12 other events, 83.5 us)

commit v2 on v0

v2 whole, which is shorter than its diff:
```python
import functools

import jax
import jax.numpy as jnp
import numpy as np
from jax import lax
from jax.experimental import pallas as pl
from jax.experimental.pallas import tpu as pltpu
from jax.sharding import PartitionSpec as P

FIELDS = 9
SLOT, BLOCK, PLACE, VISITED, LINE, HOLDS, RELAYS, NEXT, SENDS = range(FIELDS)


def flag(value):
    return value.astype(jnp.int32)


def at(turn, table, field):
    return table[turn[0] * FIELDS + field]


def device_pairs(flows, planes, lines):
    nxt = dict(flows)
    for start in [a for a in nxt if a not in nxt.values()]:
        end = start
        while end in nxt:
            end = nxt[end]
        nxt[end] = start
    pairs = []
    for z in range(planes):
        for q in range(lines):
            for k in range(2):
                to_z, to_q = nxt.get((z, q), (z, q))
                to_k = k if (z, q) in nxt else 1 - k
                pairs.append(((2 * z + k) * lines + q, (2 * to_z + to_k) * lines + to_q))
    return pairs


def diag_kernel(s_ref, block_ref, out_ref):
    rows = lax.broadcasted_iota(jnp.int32, block_ref.shape, 0)
    cols = lax.broadcasted_iota(jnp.int32, block_ref.shape, 1)
    kept = jnp.where(rows == cols, block_ref[...].astype(jnp.float32), 0.0)
    out_ref[...] = jnp.broadcast_to(jnp.sum(kept, axis=1, keepdims=True), out_ref.shape).astype(out_ref.dtype)


def diagonal(gram, core, fine=128):
    width = gram.shape[0]
    tiles = width // fine
    return pl.pallas_call(
        diag_kernel,
        grid_spec=pltpu.PrefetchScalarGridSpec(
            num_scalar_prefetch=1,
            grid=(tiles,),
            in_specs=[pl.BlockSpec((fine, fine), lambda i, s: (i, s[0] * tiles + i))],
            out_specs=pl.BlockSpec((fine, fine), lambda i, s: (i, 0)),
        ),
        out_shape=jax.ShapeDtypeStruct((width, fine), gram.dtype),
        compiler_params=pltpu.CompilerParams(dimension_semantics=("arbitrary",)),
    )(core.reshape(1), gram)


def fetch(source, target, sem):
    copy = pltpu.make_async_copy(source, target, sem)
    copy.start()
    return copy


def step_kernel(t_ref, s_ref, lam_ref, act_ref, pen, diag, beta, corr, acc, *rest, tile, rounds):
    got, (step, pay), rest = rest[:rounds], rest[rounds : rounds + 2], rest[rounds + 2 :]
    pen_v, diag_v, beta_v, corr_v, acc_v, got_v, out_v, in_sems, out_sems = rest
    field = lambda name: at(t_ref, s_ref, name)
    width = out_v.shape[0]
    parts = [pl.ds(i * tile, tile) for i in range(width // tile)]

    @pl.when(field(VISITED) == 1)
    def _():
        place = field(PLACE)
        waits = []
        for i, part in enumerate(parts):
            pairs = [(x.at[place, part], v.at[part]) for x, v in ((pen, pen_v), (diag, diag_v), (corr, corr_v), (acc, acc_v))]
            pairs.append((beta.at[field(SLOT), part], beta_v.at[part]))
            pairs += [(r.at[part], got_v.at[n, part]) for n, r in enumerate(got)]
            waits.append([fetch(x, v, in_sems.at[i, n]) for n, (x, v) in enumerate(pairs)])
        act = act_ref[field(BLOCK)]
        outs = []
        for i, part in enumerate(parts):
            for copy in waits[i]:
                copy.wait()
            beta_old, diag_now = beta_v[part], diag_v[part][:, :1].astype(jnp.float32)
            grad = corr_v[part] - acc_v[part]
            for n in range(rounds):
                grad = grad - got_v[n, part].astype(jnp.float32)
            shifted = diag_now * beta_old + grad
            size = jnp.maximum(jnp.abs(shifted) - lam_ref[...] * pen_v[part][:, :1], 0.0) / diag_now
            beta_new = jnp.where(shifted < 0.0, -size, size)
            out_v[part] = jnp.where(act == 1, beta_new - beta_old, 0.0).astype(jnp.bfloat16)
            outs += [fetch(out_v.at[part], o.at[part], out_sems.at[i, n]) for n, o in enumerate((step, pay))]
        for copy in outs:
            copy.wait()

    @pl.when((field(VISITED) == 0) & (field(SENDS) == 1))
    def _():
        waits = [fetch(acc.at[field(NEXT), part], acc_v.at[part], in_sems.at[i, 0]) for i, part in enumerate(parts)]
        outs = []
        for i, part in enumerate(parts):
            waits[i].wait()
            out_v[part] = acc_v[part].astype(jnp.bfloat16)
            outs.append(fetch(out_v.at[part], pay.at[part], out_sems.at[i, 0]))
        for copy in outs:
            copy.wait()


def soft_step(turn, table, lam, act, pen, diag, beta, corr, acc, got, tile=512):
    _, width, resp = beta.shape
    fine, rounds = pen.shape[-1], len(got)
    whole, anywhere = pl.BlockSpec(memory_space=pltpu.VMEM), pl.BlockSpec(memory_space=pl.ANY)
    parts = width // tile
    return pl.pallas_call(
        functools.partial(step_kernel, tile=tile, rounds=rounds),
        grid_spec=pltpu.PrefetchScalarGridSpec(
            num_scalar_prefetch=2,
            in_specs=[whole, whole] + [anywhere] * (5 + rounds),
            out_specs=[anywhere, anywhere],
            scratch_shapes=[
                pltpu.VMEM((width, fine), pen.dtype),
                pltpu.VMEM((width, fine), diag.dtype),
                pltpu.VMEM((width, resp), jnp.float32),
                pltpu.VMEM((width, resp), jnp.float32),
                pltpu.VMEM((width, resp), jnp.float32),
                pltpu.VMEM((rounds, width, resp), jnp.bfloat16),
                pltpu.VMEM((width, resp), jnp.bfloat16),
                pltpu.SemaphoreType.DMA((parts, 5 + rounds)),
                pltpu.SemaphoreType.DMA((parts, 2)),
            ],
        ),
        out_shape=[jax.ShapeDtypeStruct((width, resp), jnp.bfloat16)] * 2,
        compiler_params=pltpu.CompilerParams(vmem_limit_bytes=24 << 20),
        cost_estimate=pl.CostEstimate(flops=20 * resp * width, bytes_accessed=26 * resp * width, transcendentals=0),
    )(turn, table, lam, act, pen, diag, beta, corr, acc, *got)


def gram_tile(own, g_own, g_sib, first_row, first_col, target, sem, start):
    rows, cols = target.shape
    where = (pl.ds(pl.multiple_of(first_row, rows), rows), pl.ds(pl.multiple_of(first_col, cols), cols))
    if not start:
        pltpu.make_async_copy(g_own.at[where], target, sem).wait()
        return

    @pl.when(own == 1)
    def _():
        pltpu.make_async_copy(g_own.at[where], target, sem).start()

    @pl.when(own == 0)
    def _():
        pltpu.make_async_copy(g_sib.at[where], target, sem).start()


def add_block(own, g_own, g_sib, slot, x_v, tiles_v, sems, store):
    _, tile, width = tiles_v.shape
    count = width // tile
    move = lambda i, start: gram_tile(
        own, g_own, g_sib, i * tile, slot * width, tiles_v.at[i % 2], sems.at[i % 2], start
    )

    def body(i, _):
        @pl.when(i + 1 < count)
        def _():
            move(i + 1, True)

        move(i, False)
        change = jnp.dot(tiles_v[i % 2], x_v[...], preferred_element_type=jnp.float32)
        store(pl.ds(pl.multiple_of(i * tile, tile), tile), change.astype(jnp.bfloat16).astype(jnp.float32))
        return 0

    lax.fori_loop(0, count, body, 0)


def relay_kernel(t_ref, s_ref, x, step, g_own, g_sib, acc, send, x_v, acc_v, out_v, tiles_v, sems, tile_sems):
    field = lambda name: at(t_ref, s_ref, name)

    @pl.when(field(RELAYS) == 1)
    def _():
        own, slot = flag(field(NEXT) == 0), field(SLOT)
        gram_tile(own, g_own, g_sib, 0, slot * tiles_v.shape[2], tiles_v.at[0], tile_sems.at[0], True)
        waits = [fetch(x, x_v, sems.at[0]), fetch(acc.at[field(NEXT)], acc_v, sems.at[1])]
        for copy in waits:
            copy.wait()

        def store(part, change):
            out_v[part] = (acc_v[part] + change).astype(jnp.bfloat16)

        add_block(own, g_own, g_sib, slot, x_v, tiles_v, tile_sems, store)
        fetch(out_v, send, sems.at[2]).wait()

    @pl.when((field(RELAYS) == 0) & (field(VISITED) == 1))
    def _():
        fetch(step, send, sems.at[3]).wait()


def relay(turn, table, x, step, g_own, g_sib, acc, tile=1024):
    width, resp = x.shape
    anywhere = pl.BlockSpec(memory_space=pl.ANY)
    return pl.pallas_call(
        relay_kernel,
        grid_spec=pltpu.PrefetchScalarGridSpec(
            num_scalar_prefetch=2,
            in_specs=[anywhere] * 5,
            out_specs=anywhere,
            scratch_shapes=[
                pltpu.VMEM((width, resp), jnp.bfloat16),
                pltpu.VMEM((width, resp), jnp.float32),
                pltpu.VMEM((width, resp), jnp.bfloat16),
                pltpu.VMEM((2, tile, width), jnp.bfloat16),
                pltpu.SemaphoreType.DMA((4,)),
                pltpu.SemaphoreType.DMA((2,)),
            ],
        ),
        out_shape=jax.ShapeDtypeStruct((width, resp), jnp.bfloat16),
        compiler_params=pltpu.CompilerParams(vmem_limit_bytes=16 << 20),
        cost_estimate=pl.CostEstimate(
            flops=2 * resp * width * width, bytes_accessed=2 * width * width, transcendentals=0
        ),
    )(turn, table, x, step, g_own, g_sib, acc)


def update_kernel(t_ref, s_ref, g_own, g_sib, acc_in, moved_in, *rest):
    *arrived, acc, moved, x_v, acc_v, tiles_v, sems, tile_sems, out_sems = rest
    field = lambda name: at(t_ref, s_ref, name)

    @pl.when(field(LINE) == 1)
    def _():
        slot = field(SLOT)
        start = lambda j: gram_tile(
            jnp.int32(1 - j), g_own, g_sib, 0, slot * tiles_v.shape[2], tiles_v.at[0], tile_sems.at[0], True
        )
        start(0)
        sums = fetch(acc_in, acc_v, sems.at[0])
        for n, r in enumerate(arrived):

            @pl.when(field(HOLDS) == n)
            def _():
                fetch(r, x_v, sems.at[1]).wait()

        kept = fetch(x_v, moved.at[slot], sems.at[2])
        sums.wait()
        outs = []
        for j in range(2):

            def store(part, change):
                acc_v[j, part] = acc_v[j, part] + change

            if j:
                start(1)
            add_block(jnp.int32(1 - j), g_own, g_sib, slot, x_v, tiles_v, tile_sems, store)
            outs.append(fetch(acc_v.at[j], acc.at[j], out_sems.at[j]))
        kept.wait()
        for copy in outs:
            copy.wait()


def update(turn, table, g_own, g_sib, acc, moved, arrived, tile=1024):
    _, width, resp = acc.shape
    anywhere = pl.BlockSpec(memory_space=pl.ANY)
    return pl.pallas_call(
        update_kernel,
        grid_spec=pltpu.PrefetchScalarGridSpec(
            num_scalar_prefetch=2,
            in_specs=[anywhere] * (4 + len(arrived)),
            out_specs=[anywhere, anywhere],
            scratch_shapes=[
                pltpu.VMEM((width, resp), jnp.bfloat16),
                pltpu.VMEM((2, width, resp), jnp.float32),
                pltpu.VMEM((2, tile, width), jnp.bfloat16),
                pltpu.SemaphoreType.DMA((3,)),
                pltpu.SemaphoreType.DMA((2,)),
                pltpu.SemaphoreType.DMA((2,)),
            ],
        ),
        out_shape=[jax.ShapeDtypeStruct(acc.shape, acc.dtype), jax.ShapeDtypeStruct(moved.shape, moved.dtype)],
        input_output_aliases={4: 0, 5: 1},
        compiler_params=pltpu.CompilerParams(vmem_limit_bytes=16 << 20),
        cost_estimate=pl.CostEstimate(
            flops=4 * resp * width * width, bytes_accessed=4 * width * width, transcendentals=0
        ),
    )(turn, table, g_own, g_sib, acc, moved, *arrived)


def start_kernel(k_ref, beta_ref, half_ref, flat_ref):
    resp = half_ref.shape[1]
    for lam in range(2):

        @pl.when(k_ref[0] == lam)
        def _():
            half_ref[...] = beta_ref[:, lam, :]

        flat_ref[:, lam * resp : (lam + 1) * resp] = beta_ref[:, lam, :].astype(flat_ref.dtype)


def start_beta(core, beta, tile=512):
    rows, lams, resp = beta.shape
    return pl.pallas_call(
        start_kernel,
        grid_spec=pltpu.PrefetchScalarGridSpec(
            num_scalar_prefetch=1,
            grid=(rows // tile,),
            in_specs=[pl.BlockSpec((tile, lams, resp), lambda i, k: (i, 0, 0))],
            out_specs=[
                pl.BlockSpec((tile, resp), lambda i, k: (i, 0)),
                pl.BlockSpec((tile, lams * resp), lambda i, k: (i, 0)),
            ],
        ),
        out_shape=[
            jax.ShapeDtypeStruct((rows, resp), beta.dtype),
            jax.ShapeDtypeStruct((rows, lams * resp), jnp.bfloat16),
        ],
    )(core, beta)


def join_kernel(k_ref, mine_ref, other_ref, *rest):
    *base, out_ref = rest
    for lam in range(2):
        value = jnp.where(k_ref[0] == lam, mine_ref[...], other_ref[...]).astype(out_ref.dtype)
        out_ref[:, lam, :] = value + base[0][:, lam, :] if base else value


def join(core, mine, other, base=(), tile=512):
    rows, resp = mine.shape
    flat = pl.BlockSpec((tile, resp), lambda i, k: (i, 0))
    deep = pl.BlockSpec((tile, 2, resp), lambda i, k: (i, 0, 0))
    return pl.pallas_call(
        join_kernel,
        grid_spec=pltpu.PrefetchScalarGridSpec(
            num_scalar_prefetch=1, grid=(rows // tile,), in_specs=[flat, flat] + [deep] * len(base), out_specs=deep
        ),
        out_shape=jax.ShapeDtypeStruct((rows, 2, resp), jnp.float32),
        cost_estimate=pl.CostEstimate(flops=4 * rows * resp, bytes_accessed=20 * rows * resp, transcendentals=0),
    )(core, mine, other, *base)


def routes(p, pn, planes, lines):
    rest_q = [c for c in range(lines) if c not in (p, pn)]
    rest_z = sorted([c for c in range(planes) if c not in (p, pn)], key=lambda c: abs(c - p) - abs(c - pn))
    if p == pn:
        return [([((p, p), (c, p)), ((p, c), (p, p))], c, p) for c in rest_z]
    first = ([((p, p), (pn, p))] + [((pn, c), (pn, pn)) for c in rest_q[:1]], pn, p)
    last = ([((pn, p), (pn, pn))] + [((p, p), (c, p)) for c in rest_z[:1]], rest_z[0] if rest_z else pn, p)
    between = []
    for line, plane in zip(rest_q[1:], rest_z[1:]):
        source = p if abs(plane - p) < abs(plane - pn) else pn
        between.append(([((source, p), (plane, p)), ((pn, line), (pn, pn))], plane, source))
    return [first, *between, last]


def per_device(planes, lines, gram, corr, beta_start, lambdas, penalty, strong, active, order):
    width = corr.shape[0]
    lam_count, phenos = beta_start.shape[1:]
    cols = lam_count * phenos
    half = cols // 2
    row = lax.axis_index("row")
    z, k, q = row // 2, row % 2, lax.axis_index("col")
    swap = [(r * lines + c, (r ^ 1) * lines + c) for r in range(2 * planes) for c in range(lines)]
    permute = lambda x, pairs: lax.ppermute(x, ("row", "col"), pairs)
    pair_of = lambda mine: jnp.stack([mine, permute(mine, swap)])
    core = k.reshape(1)

    def gather_col(x):
        return lax.all_to_all(jnp.broadcast_to(x[None], (lines, *x.shape)), "col", 0, 0)

    g_sib = permute(gram, swap)

    beta_half, flat = start_beta(core, beta_start)
    product = jnp.dot(gram, flat, preferred_element_type=jnp.float32)
    other = permute(lax.dynamic_slice_in_dim(product, (1 - k) * half, half, 1), swap)
    shares = jnp.stack([lax.dynamic_slice_in_dim(product, k * half, half, 1), other])

    fine = 128
    wanted = penalty.reshape(-1, fine)[strong // fine]
    chosen = lax.broadcasted_iota(jnp.int32, wanted.shape, 1) == (strong % fine)[:, None]
    pen_own = jnp.broadcast_to(jnp.sum(jnp.where(chosen, wanted, 0.0), axis=1, keepdims=True), wanted.shape)
    diag_own = diagonal(gram, k, fine)
    pen, diag = pair_of(pen_own), pair_of(diag_own)

    corr = pair_of(corr)
    beta0 = beta_half.reshape(2, width, half)
    lam = lax.dynamic_slice_in_dim(jnp.repeat(lambdas, phenos), k * half, half)[None, :]
    act = lax.dynamic_slice_in_dim(jnp.repeat(active.T, phenos, axis=1), k * half, half, 1)[:, None, :]

    holds = np.zeros((planes, planes, planes), np.int32)
    for p in range(planes):
        for pn in range(planes):
            for n, (_, plane, _) in enumerate(routes(p, pn, planes, lines)):
                holds[p, pn, plane] = n + 1
            holds[p, pn, p] = 0
    after = jnp.concatenate([order, order[-1:]])
    order = jnp.concatenate([order[:1], order])
    real = flag(jnp.arange(order.shape[0]) > 0)
    pair, pair_n, slot_n = order // 2, after // 2, after % 2
    held = lax.dynamic_index_in_dim(jnp.asarray(holds), z, 2, keepdims=False)[pair, pair_n]
    line = flag(q == pair) * real
    table = jnp.stack(
        [
            order % 2,
            order,
            (order % 2) ^ k,
            flag(z == pair) * line,
            line,
            held,
            flag((z == pair_n) & (pair != pair_n)) * line,
            slot_n ^ k,
            flag(z == pair_n),
        ],
        axis=1,
    ).reshape(-1)
    which = pair * planes + pair_n

    def branch(p, pn):
        plan = routes(p, pn, planes, lines)
        send = lambda payload, flows: permute(payload, device_pairs(flows, planes, lines))

        def run(operands):
            turn, step, pay, acc = operands
            if p == pn:
                return tuple(send(pay, flows) for flows, _, _ in plan)
            at_pn = (z == pn) & (q == p)
            first = send(pay, plan[0][0])
            out = relay(turn, table, first, step, gram, g_sib, acc)
            late, late_pay, out = lax.optimization_barrier((first, pay, out))
            between = [
                send(pay if source == p else jnp.where(at_pn, late, late_pay), flows) for flows, _, source in plan[1:-1]
            ]
            return (first, *between, send(out, plan[-1][0]))

        return run

    branches = [branch(p, pn) for p in range(planes) for pn in range(planes)]

    def visit(count, carry):
        acc, moved, got = carry
        turn = count.reshape(1)
        step, pay = soft_step(turn, table, lam, act, pen, diag, beta0, corr, acc, got)
        got = lax.switch(which[count], branches, (turn, step, pay, acc))
        acc, moved = update(turn, table, gram, g_sib, acc, moved, (step, *got))
        return acc, moved, got

    empty = jnp.zeros((2, width, half), jnp.bfloat16)
    carry = (shares, empty, (empty[0],) * (planes - 1))
    acc, moved, _ = lax.fori_loop(0, order.shape[0], visit, carry)

    part = width // lines
    acc, moved_other = lax.optimization_barrier((acc, permute(moved, swap)))
    share = lax.all_to_all(acc.reshape(2, lines, part, half).swapaxes(0, 1), "col", 0, 0)
    beta = join(
        core, moved.reshape(2 * width, half), moved_other.reshape(2 * width, half), (beta_start,)
    )
    share = lax.dynamic_slice_in_dim(corr, q * part, part, 1) - jnp.sum(share, axis=0)
    final = gather_col(share.astype(jnp.bfloat16))
    other = permute(final[:, 1].reshape(width, half), swap)
    return beta, join(core, final[:, 0].reshape(width, half), other)


def solution(mesh):
    planes, lines = mesh.shape["row"] // 2, mesh.shape["col"]
    in_specs = (P("row", "col"), P("row", None), P("col", None, None), P(), P(), P("row"), P(), P())
    out_specs = (P("col", None, None), P("row", None, None))
    return jax.shard_map(
        functools.partial(per_device, planes, lines),
        mesh=mesh, in_specs=in_specs, out_specs=out_specs, check_vma=False,
    )
```

time: 1300 us -> 587 us (0.45)
  waiting for transfers between devices: 922 us -> 111 us
  starting transfers between devices: 0.71 us -> 315 us
  other arithmetic: 165 us -> 19.9 us
  local copies, waits for them, and re-layouts: 125 us -> 29 us
  Pallas kernels: 0 us -> 71.9 us
  loops' own time: 42.4 us -> 6.54 us
  blocking collectives: 0 us -> 16.2 us
  between operations: 13.9 us -> 0.79 us
    psum x17 -> x0, waiting for transfers between devices: 922 us -> none  [the longest x16 922 us: broadcast(): return lax.psum(block, axis)]
    ppermute x0 -> x34, starting transfers between devices: none -> 277 us  [per_device(): permute = lambda x, pairs: lax.ppermute(x, ('row', 'col'), pairs)]
    select_n x24 -> x5, other arithmetic: 114 us -> 4.47 us  [the longest x4 4.45 us: run(): jnp.where(at_pn, late, late_pay)]
    ppermute x0 -> x34, waiting for transfers between devices: none -> 86.2 us  [per_device(): permute = lambda x, pairs: lax.ppermute(x, ('row', 'col'), pairs)]
    pallas_call x0 -> x28, Pallas kernels: none -> 71.9 us  [the longest x9 27.2 us: update(): pl.pallas_call(update_kernel, grid_spec=pltpu.PrefetchScalarGridSpec(num_...]
    gather x3 -> x2, local copies, waits for them, and re-layouts: 76.8 us -> 8.36 us  [the longest x1 7.62 us: per_device(): wanted = penalty.reshape(-1, fine)[strong // fine]]
    all_to_all x0 -> x1, starting transfers between devices: none -> 37.8 us  [per_device(): lax.all_to_all(acc.reshape(2, lines, part, half).swapaxes(0, 1), 'col', 0...]
    another operation x9 -> x10, loops' own time: 42.4 us -> 6.54 us  [the longest x1 6.06 us: per_device(): acc, moved, _ = lax.fori_loop(0, order.shape[0], visit, carry)]
  transfers between devices with their start and end apart: 17 -> 35, of which waited for: 16 -> 23; matrix products, arithmetic and copies ran while one was open for 7% -> 7% of each run, Pallas kernels for 0% -> 5%
where the time goes in v2:
time: 587 us; the launch traced here: 583 us
  starting transfers between devices  315 us (54%)
  waiting for transfers between devices  111 us (19%)
  Pallas kernels  71.9 us (12%)
  local copies, waits for them, and re-layouts  29 us (5%)
  other arithmetic  19.9 us (3%)
  blocking collectives  16.2 us (3%)
  matrix products  12.3 us (2%)
  loops' own time  6.54 us (1%)
    ppermute x34, starting transfers between devices, per_device(): permute = lambda x, pairs: lax.ppermute(x, ('row', 'col'), pairs)  277 us
    ppermute x34, waiting for transfers between devices, per_device(): permute = lambda x, pairs: lax.ppermute(x, ('row', 'col'), pairs)  86.2 us
    all_to_all x1, starting transfers between devices, per_device(): lax.all_to_all(acc.reshape(2, lines, part, half).swapaxes(0, 1), 'col', 0...  37.8 us
    pallas_call x9, Pallas kernels, update(): pl.pallas_call(update_kernel, grid_spec=pltpu.PrefetchScalarGridSpec(num_...  27.2 us
    all_to_all x1, waiting for transfers between devices, per_device(): lax.all_to_all(acc.reshape(2, lines, part, half).swapaxes(0, 1), 'col', 0...  25.2 us
    all_to_all x1, blocking collectives, gather_col(): lax.all_to_all(jnp.broadcast_to(x[None], (lines, *x.shape)), 'col', 0, 0)  16.2 us
    pallas_call x2, Pallas kernels, join(): pl.pallas_call(join_kernel, grid_spec=pltpu.PrefetchScalarGridSpec(num_sc...  13.1 us
    dot_general x1, matrix products, per_device(): product = jnp.dot(gram, flat, preferred_element_type=jnp.float32)  12.3 us
  transfers between devices with their start and end apart: 35, of which 23 were waited for; matrix products, arithmetic and copies ran while one was open for 7% of the time, Pallas kernels for 5%

profile of v2, /device:TPU:8, one launch (start us, length us, event | category | flops | bytes accessed | tf_op | source)
XLA Modules:
  0.0 582.9 jit_solution(14861077909359481620)
XLA Ops:
  0.8 8.8 %shard_map.104 = (f32[4096,128]{1,0:T(8,128)}, bf16[4096,256]{1,0:T(8,128)(2,1)}) custom-call(s32[1]{0:T(128)} %bitcast.2.k_ref.s_ref, f32[4096,2,128]{2,1,0:T(2,128)} %rest_0_.1), custom_call_target="tpu_custom_call" | custom-call | tf_op jit(solution)/shard_map/pallas_call | solution.py:302
  9.5 12.3 %fusion.17 = f32[256,2048]{1,0:T(8,128)} fusion(bf16[4096,256]{1,0:T(8,128)(2,1)} %get-tuple-element.628, bf16[2048,4096]{1,0:T(8,128)(2,1)} %block_ref.1), kind=kOutput, calls=%fused_computation.81 | convolution fusion | flops 4294967296 | bytes 20971520 | tf_op jit(solution)/shard_map/dot_general | solution.py:373
  24.9 8.8 %shard_map.105 = bf16[2048,128]{1,0:T(8,128)(2,1)} custom-call(s32[1]{0:T(128)} %bitcast.2.k_ref.s_ref, bf16[2048,4096]{1,0:T(8,128)(2,1)} %block_ref.1), custom_call_target="tpu_custom_call" | custom-call | tf_op jit(solution)/shard_map/pallas_call | solution.py:50
  33.9 7.6 %gather_fusion.1 = f32[2048,128]{1,0:T(8,128)} fusion(f32[2048,128]{1,0:T(8,128)S(1)} %bitcast.48, s32[2048]{0:T(1024)S(1)} %get-tuple-element.755), kind=kCustom, calls=%fused_computation.1 | custom fusion | bytes 2105344 | tf_op jit(solution)/shard_map/gather | solution.py:378
  66.1 416.7 %while.21 = (s32[]{:T(128)}, f32[2,2048,128]{2,1,0:T(8,128)S(1)}, bf16[2,2048,128]{2,1,0:T(8,128)(2,1)}, bf16[2048,128]{1,0:T(8,128)(2,1)}, bf16[2048,128]{1,0:T...) while((s32[]{:T(128)}, f32[2,2048,128]{2,1,0:T(8,128)S(1)}, ...), condition=%wide.region_18.19_spmd, body=%wide.region_1.18_spmd.sunk | while | flops 3226730496 | bytes 39846400 | solution.py:448
  68.3 10.4 %conditional.2 = (bf16[2048,128]{1,0:T(8,128)(2,1)}, bf16[2048,128]{1,0:T(8,128)(2,1)}, bf16[2048,128]{1,0:T(8,128)(2,1)}) conditional(s32[]{:T(128)} %bitcast.47, bf16[2048,128]{1,0:T(8,128)(2,1)} %get-tuple-element.881, (bf16[2048,128]{1,0:T(8,128)(2,1)}, s32[]{:T(128)}, s32[]{:T(128)}, s32[1]{0:T(128)}, ...), branch_computations={%region_2.2_spmd, %region_3.3_spmd, %region_4.4_spmd, %region_5.5_... | conditional | flops 1074003968 | bytes 16253094 | solution.py:442
  68.4 6.9 %collective-permute-start.15 = (bf16[2048,128]{1,0:T(8,128)(2,1)}, bf16[2048,128]{1,0:T(8,128)(2,1)}, u32[]{:S(2)}, u32[]{:S(2)}) collective-permute-start(bf16[2048,128]{1,0:T(8,128)(2,1)} %param.15), channel_id=1, source_target_pairs={{0,4},{4,0},{1,5},{5,1},{2,6},{6,2},{3,24},{7,28},{8,12},{12,8},{9... | collective-permute-start | bytes 1572872 | tf_op jit(solution)/shard_map/while/body/eval_jaxpr/cond/branch_15_fun/ppermute | solution.py:363
  82.5 61.6 %conditional.2 = (bf16[2048,128]{1,0:T(8,128)(2,1)}, bf16[2048,128]{1,0:T(8,128)(2,1)}, bf16[2048,128]{1,0:T(8,128)(2,1)}) conditional(s32[]{:T(128)} %bitcast.47, bf16[2048,128]{1,0:T(8,128)(2,1)} %get-tuple-element.881, (bf16[2048,128]{1,0:T(8,128)(2,1)}, s32[]{:T(128)}, s32[]{:T(128)}, s32[1]{0:T(128)}, ...), branch_computations={%region_2.2_spmd, %region_3.3_spmd, %region_4.4_spmd, %region_5.5_... | conditional | flops 1074003968 | bytes 16253094 | solution.py:442
  84.1 13.0 %collective-permute-done.42.x = bf16[2048,128]{1,0:T(8,128)(2,1)} collective-permute-done((bf16[2048,128]{1,0:T(8,128)(2,1)}, bf16[2048,128]{1,0:T(8,128)(2,1)}, u32[]{:S(2)}, u32[]{:S(2)}) %collective-permute-start.42) | collective-permute-done | bytes 524320 | tf_op jit(solution)/shard_map/while/body/eval_jaxpr/cond/branch_13_fun/ppermute | solution.py:363
  98.8 42.8 %collective-permute-start.43 = (bf16[2048,128]{1,0:T(8,128)(2,1)S(1)}, bf16[2048,128]{1,0:T(8,128)(2,1)}, u32[]{:S(2)}, u32[]{:S(2)}) collective-permute-start(bf16[2048,128]{1,0:T(8,128)(2,1)S(1)} %broadcast_select_fusion.8), channel_id=1, source_target_pairs={{0,4},{4,0},{1,5},{5,1},{2,6},{6,2},{3,11},{7,15},{8,12},{12,8},{9... | collective-permute-start | bytes 1572872 | tf_op jit(solution)/shard_map/while/body/eval_jaxpr/cond/branch_13_fun/ppermute | solution.py:363
  146.9 53.1 %conditional.2 = (bf16[2048,128]{1,0:T(8,128)(2,1)}, bf16[2048,128]{1,0:T(8,128)(2,1)}, bf16[2048,128]{1,0:T(8,128)(2,1)}) conditional(s32[]{:T(128)} %bitcast.47, bf16[2048,128]{1,0:T(8,128)(2,1)} %get-tuple-element.881, (bf16[2048,128]{1,0:T(8,128)(2,1)}, s32[]{:T(128)}, s32[]{:T(128)}, s32[1]{0:T(128)}, ...), branch_computations={%region_2.2_spmd, %region_3.3_spmd, %region_4.4_spmd, %region_5.5_... | conditional | flops 1074003968 | bytes 16253094 | solution.py:442
  151.4 46.9 %collective-permute-start.29 = (bf16[2048,128]{1,0:T(8,128)(2,1)S(1)}, bf16[2048,128]{1,0:T(8,128)(2,1)}, u32[]{:S(2)}, u32[]{:S(2)}) collective-permute-start(bf16[2048,128]{1,0:T(8,128)(2,1)S(1)} %branch_6_fun.1), channel_id=1, source_target_pairs={{0,4},{4,0},{1,9},{5,13},{2,6},{6,2},{3,7},{7,3},{8,12},{12,8},{9,... | collective-permute-start | bytes 1572872 | tf_op jit(solution)/shard_map/while/body/eval_jaxpr/cond/branch_6_fun/ppermute | solution.py:363
  203.7 42.1 %conditional.2 = (bf16[2048,128]{1,0:T(8,128)(2,1)}, bf16[2048,128]{1,0:T(8,128)(2,1)}, bf16[2048,128]{1,0:T(8,128)(2,1)}) conditional(s32[]{:T(128)} %bitcast.47, bf16[2048,128]{1,0:T(8,128)(2,1)} %get-tuple-element.881, (bf16[2048,128]{1,0:T(8,128)(2,1)}, s32[]{:T(128)}, s32[]{:T(128)}, s32[1]{0:T(128)}, ...), branch_computations={%region_2.2_spmd, %region_3.3_spmd, %region_4.4_spmd, %region_5.5_... | conditional | flops 1074003968 | bytes 16253094 | solution.py:442
  203.8 22.5 %collective-permute-start.36 = (bf16[2048,128]{1,0:T(8,128)(2,1)}, bf16[2048,128]{1,0:T(8,128)(2,1)}, u32[]{:S(2)}, u32[]{:S(2)}) collective-permute-start(bf16[2048,128]{1,0:T(8,128)(2,1)} %get-tuple-element.548), channel_id=1, source_target_pairs={{0,4},{4,0},{1,5},{5,1},{2,6},{6,2},{3,7},{7,3},{8,9},{12,13},{9,8... | collective-permute-start | bytes 1572872 | tf_op jit(solution)/shard_map/while/body/eval_jaxpr/cond/branch_9_fun/ppermute | solution.py:363
  226.3 12.0 %collective-permute-done.36.x = bf16[2048,128]{1,0:T(8,128)(2,1)} collective-permute-done((bf16[2048,128]{1,0:T(8,128)(2,1)}, bf16[2048,128]{1,0:T(8,128)(2,1)}, u32[]{:S(2)}, u32[]{:S(2)}) %collective-permute-start.36) | collective-permute-done | bytes 524320 | tf_op jit(solution)/shard_map/while/body/eval_jaxpr/cond/branch_9_fun/ppermute | solution.py:363
  256.6 103.9 %conditional.2 = (bf16[2048,128]{1,0:T(8,128)(2,1)}, bf16[2048,128]{1,0:T(8,128)(2,1)}, bf16[2048,128]{1,0:T(8,128)(2,1)}) conditional(s32[]{:T(128)} %bitcast.47, bf16[2048,128]{1,0:T(8,128)(2,1)} %get-tuple-element.881, (bf16[2048,128]{1,0:T(8,128)(2,1)}, s32[]{:T(128)}, s32[]{:T(128)}, s32[1]{0:T(128)}, ...), branch_computations={%region_2.2_spmd, %region_3.3_spmd, %region_4.4_spmd, %region_5.5_... | conditional | flops 1074003968 | bytes 16253094 | solution.py:442
  256.6 69.3 %collective-permute-start = (bf16[2048,128]{1,0:T(8,128)(2,1)}, bf16[2048,128]{1,0:T(8,128)(2,1)}, u32[]{:S(2)}, u32[]{:S(2)}) collective-permute-start(bf16[2048,128]{1,0:T(8,128)(2,1)} %param), channel_id=1, source_target_pairs={{0,8},{4,12},{1,0},{5,4},{2,6},{6,2},{3,7},{7,3},{8,1},{12,5},{9,1... | collective-permute-start | bytes 1572872 | tf_op jit(solution)/shard_map/while/body/eval_jaxpr/cond/branch_0_fun/ppermute | solution.py:363
  325.8 5.7 collective-permute-start.1
  337.3 23.1 %collective-permute-done = bf16[2048,128]{1,0:T(8,128)(2,1)} collective-permute-done((bf16[2048,128]{1,0:T(8,128)(2,1)}, bf16[2048,128]{1,0:T(8,128)(2,1)}, u32[]{:S(2)}, u32[]{:S(2)}) %collective-permute-start) | collective-permute-done | bytes 524320 | tf_op jit(solution)/shard_map/while/body/eval_jaxpr/cond/branch_0_fun/ppermute | solution.py:363
  360.4 11.4 %eval_jaxpr.11 = (f32[2,2048,128]{2,1,0:T(8,128)S(1)}, bf16[2,2048,128]{2,1,0:T(8,128)(2,1)}) custom-call(s32[1]{0:T(128)} %bitcast.46.t_ref, s32[81]{0:T(128)S(1)} %get-tuple-element.983.s_ref, bf16[2048,4096]{1,0:T(8,128)(2,1)} %get-tuple-element.993.g_own, ...), custom_call_target="tpu_custom_call", output_to_operand_aliasing={{0}: (4, {}), {1}: (5, {})} | custom-call | flops 2147483648 | bytes 16777216 | tf_op jit(solution)/shard_map/while/body/eval_jaxpr/pallas_call | solution.py:265
  374.1 41.7 %conditional.2 = (bf16[2048,128]{1,0:T(8,128)(2,1)}, bf16[2048,128]{1,0:T(8,128)(2,1)}, bf16[2048,128]{1,0:T(8,128)(2,1)}) conditional(s32[]{:T(128)} %bitcast.47, bf16[2048,128]{1,0:T(8,128)(2,1)} %get-tuple-element.881, (bf16[2048,128]{1,0:T(8,128)(2,1)}, s32[]{:T(128)}, s32[]{:T(128)}, s32[1]{0:T(128)}, ...), branch_computations={%region_2.2_spmd, %region_3.3_spmd, %region_4.4_spmd, %region_5.5_... | conditional | flops 1074003968 | bytes 16253094 | solution.py:442
  382.9 20.2 %collective-permute-start.23 = (bf16[2048,128]{1,0:T(8,128)(2,1)S(1)}, bf16[2048,128]{1,0:T(8,128)(2,1)}, u32[]{:S(2)}, u32[]{:S(2)}) collective-permute-start(bf16[2048,128]{1,0:T(8,128)(2,1)S(1)} %branch_2_fun.1), channel_id=1, source_target_pairs={{0,8},{4,12},{1,5},{5,1},{2,6},{6,2},{3,7},{7,3},{8,0},{12,4},{9,1... | collective-permute-start | bytes 1572872 | tf_op jit(solution)/shard_map/while/body/eval_jaxpr/cond/branch_2_fun/ppermute | solution.py:363
  403.0 12.7 %collective-permute-done.23 = bf16[2048,128]{1,0:T(8,128)(2,1)} collective-permute-done((bf16[2048,128]{1,0:T(8,128)(2,1)S(1)}, bf16[2048,128]{1,0:T(8,128)(2,1)}, u32[]{:S(2)}, u32[]{:S(2)}) %collective-permute-start.23) | collective-permute-done | bytes 524320 | tf_op jit(solution)/shard_map/while/body/eval_jaxpr/cond/branch_2_fun/ppermute | solution.py:363
  415.7 11.5 %eval_jaxpr.11 = (f32[2,2048,128]{2,1,0:T(8,128)S(1)}, bf16[2,2048,128]{2,1,0:T(8,128)(2,1)}) custom-call(s32[1]{0:T(128)} %bitcast.46.t_ref, s32[81]{0:T(128)S(1)} %get-tuple-element.983.s_ref, bf16[2048,4096]{1,0:T(8,128)(2,1)} %get-tuple-element.993.g_own, ...), custom_call_target="tpu_custom_call", output_to_operand_aliasing={{0}: (4, {}), {1}: (5, {})} | custom-call | flops 2147483648 | bytes 16777216 | tf_op jit(solution)/shard_map/while/body/eval_jaxpr/pallas_call | solution.py:265
  429.4 17.8 %conditional.2 = (bf16[2048,128]{1,0:T(8,128)(2,1)}, bf16[2048,128]{1,0:T(8,128)(2,1)}, bf16[2048,128]{1,0:T(8,128)(2,1)}) conditional(s32[]{:T(128)} %bitcast.47, bf16[2048,128]{1,0:T(8,128)(2,1)} %get-tuple-element.881, (bf16[2048,128]{1,0:T(8,128)(2,1)}, s32[]{:T(128)}, s32[]{:T(128)}, s32[1]{0:T(128)}, ...), branch_computations={%region_2.2_spmd, %region_3.3_spmd, %region_4.4_spmd, %region_5.5_... | conditional | flops 1074003968 | bytes 16253094 | solution.py:442
  432.4 13.1 %collective-permute-start.14 = (bf16[2048,128]{1,0:T(8,128)(2,1)S(1)}, bf16[2048,128]{1,0:T(8,128)(2,1)}, u32[]{:S(2)}, u32[]{:S(2)}) collective-permute-start(bf16[2048,128]{1,0:T(8,128)(2,1)S(1)} %branch_11_fun.1), channel_id=1, source_target_pairs={{0,4},{4,0},{1,5},{5,1},{2,18},{6,22},{3,7},{7,3},{8,12},{12,8},{9... | collective-permute-start | bytes 1572872 | tf_op jit(solution)/shard_map/while/body/eval_jaxpr/cond/branch_11_fun/ppermute | solution.py:363
  450.0 32.2 %conditional.2 = (bf16[2048,128]{1,0:T(8,128)(2,1)}, bf16[2048,128]{1,0:T(8,128)(2,1)}, bf16[2048,128]{1,0:T(8,128)(2,1)}) conditional(s32[]{:T(128)} %bitcast.47, bf16[2048,128]{1,0:T(8,128)(2,1)} %get-tuple-element.881, (bf16[2048,128]{1,0:T(8,128)(2,1)}, s32[]{:T(128)}, s32[]{:T(128)}, s32[1]{0:T(128)}, ...), branch_computations={%region_2.2_spmd, %region_3.3_spmd, %region_4.4_spmd, %region_5.5_... | conditional | flops 1074003968 | bytes 16253094 | solution.py:442
  450.1 28.8 %collective-permute-start.15 = (bf16[2048,128]{1,0:T(8,128)(2,1)}, bf16[2048,128]{1,0:T(8,128)(2,1)}, u32[]{:S(2)}, u32[]{:S(2)}) collective-permute-start(bf16[2048,128]{1,0:T(8,128)(2,1)} %param.15), channel_id=1, source_target_pairs={{0,4},{4,0},{1,5},{5,1},{2,6},{6,2},{3,24},{7,28},{8,12},{12,8},{9... | collective-permute-start | bytes 1572872 | tf_op jit(solution)/shard_map/while/body/eval_jaxpr/cond/branch_15_fun/ppermute | solution.py:363
  487.4 37.8 %all-to-all-start = ((f32[4,2,512,128]{3,2,1,0:T(8,128)}), f32[4,2,512,128]{3,2,1,0:T(8,128)S(1)}, u32[]{:S(2)}, u32[]{:S(2)}) async-start(f32[4,2,512,128]{3,2,1,0:T(8,128)} %copy.21), calls=%async_computation | async-start | bytes 4194304 | tf_op jit(solution)/shard_map/all_to_all | solution.py:452
  525.2 25.2 %all-to-all-done = f32[4,2,512,128]{3,2,1,0:T(8,128)S(1)} async-done(((f32[4,2,512,128]{3,2,1,0:T(8,128)}), f32[4,2,512,128]{3,2,1,0:T(8,128)S(1)}, u32[]{:S(2)}, u32[]{:S(2)}) %all-to-all-start) | async-done | bytes 2097184 | tf_op jit(solution)/shard_map/all_to_all | solution.py:452
  551.8 16.2 %all_to_all.10 = bf16[4,2,512,128]{3,2,1,0:T(8,128)(2,1)S(1)} all-to-all(bf16[4,2,512,128]{3,2,1,0:T(8,128)(2,1)S(1)} %broadcast_in_dim.45), channel_id=1, replica_groups=mesh['row'=8,'col'=4] {'col'}, dimensions={0} | all-to-all | bytes 2097152 | tf_op jit(solution)/shard_map/all_to_all | solution.py:368
  568.9 9.0 %shard_map.106 = f32[4096,2,128]{2,1,0:T(2,128)} custom-call(s32[1]{0:T(128)} %bitcast.2.k_ref.s_ref, bf16[4096,128]{1,0:T(8,128)(2,1)S(1)} %bitcast.51, bf16[4096,128]{1,0:T(8,128)(2,1)} %bitcast.27.other_ref, f32[4096,2,128]{2,1,0:T(2,128)} %rest_0_.1), custom_call_target="tpu_custom_call" | custom-call | flops 2097152 | bytes 10485760 | tf_op jit(solution)/shard_map/pallas_call | solution.py:331
  (144 shorter events, 115.1 us)
Async XLA Ops:
  0.6 61.7 %collective-permute-start.52 = (bf16[2048,4096]{1,0:T(8,128)(2,1)}, bf16[2048,4096]{1,0:T(8,128)(2,1)}, u32[]{:S(2)}, u32[]{:S(2)}) collective-permute-start(bf16[2048,4096]{1,0:T(8,128)(2,1)} %block_ref.1), channel_id=1, source_target_pairs={{0,4},{1,5},{2,6},{3,7},{4,0},{5,1},{6,2},{7,3},{8,12},{9,13},{10,... | collective-permute-start | bytes 50331656 | tf_op jit(solution)/shard_map/ppermute | solution.py:363
  24.5 27.0 %collective-permute-start.48 = (f32[2048,128]{0,1:T(8,128)}, f32[2048,128]{0,1:T(8,128)}, u32[]{:S(2)}, u32[]{:S(2)}) collective-permute-start(f32[2048,128]{0,1:T(8,128)} %get-tuple-element.751), channel_id=1, source_target_pairs={{0,4},{1,5},{2,6},{3,7},{4,0},{5,1},{6,2},{7,3},{8,12},{9,13},{10,... | collective-permute-start | bytes 3145736 | tf_op jit(solution)/shard_map/ppermute | solution.py:363
  33.7 16.8 %collective-permute-start.50 = (bf16[2048,128]{1,0:T(8,128)(2,1)}, bf16[2048,128]{1,0:T(8,128)(2,1)S(1)}, u32[]{:S(2)}, u32[]{:S(2)}) collective-permute-start(bf16[2048,128]{1,0:T(8,128)(2,1)} %shard_map.105), channel_id=1, source_target_pairs={{0,4},{1,5},{2,6},{3,7},{4,0},{5,1},{6,2},{7,3},{8,12},{9,13},{10,... | collective-permute-start | bytes 1572872 | tf_op jit(solution)/shard_map/ppermute | solution.py:363
  44.7 11.5 %collective-permute-start.49 = (f32[2048,128]{1,0:T(8,128)}, f32[2048,128]{1,0:T(8,128)}, u32[]{:S(2)}, u32[]{:S(2)}) collective-permute-start(f32[2048,128]{1,0:T(8,128)} %broadcast_in_dim.44), channel_id=1, source_target_pairs={{0,4},{1,5},{2,6},{3,7},{4,0},{5,1},{6,2},{7,3},{8,12},{9,13},{10,... | collective-permute-start | bytes 3145736 | tf_op jit(solution)/shard_map/ppermute | solution.py:363
  45.1 14.3 %collective-permute-start.51 = (f32[2048,128]{1,0:T(8,128)}, f32[2048,128]{1,0:T(8,128)}, u32[]{:S(2)}, u32[]{:S(2)}) collective-permute-start(f32[2048,128]{1,0:T(8,128)} %param.28), channel_id=1, source_target_pairs={{0,4},{1,5},{2,6},{3,7},{4,0},{5,1},{6,2},{7,3},{8,12},{9,13},{10,... | collective-permute-start | bytes 3145736 | tf_op jit(solution)/shard_map/ppermute | solution.py:363
  68.4 8.8 %collective-permute-start.15 = (bf16[2048,128]{1,0:T(8,128)(2,1)}, bf16[2048,128]{1,0:T(8,128)(2,1)}, u32[]{:S(2)}, u32[]{:S(2)}) collective-permute-start(bf16[2048,128]{1,0:T(8,128)(2,1)} %param.15), channel_id=1, source_target_pairs={{0,4},{4,0},{1,5},{5,1},{2,6},{6,2},{3,24},{7,28},{8,12},{12,8},{9... | collective-permute-start | bytes 1572872 | tf_op jit(solution)/shard_map/while/body/eval_jaxpr/cond/branch_15_fun/ppermute | solution.py:363
  75.3 2.6 collective-permute-start.16
  75.5 3.2 collective-permute-start.17
  82.5 14.6 %collective-permute-start.42 = (bf16[2048,128]{1,0:T(8,128)(2,1)}, bf16[2048,128]{1,0:T(8,128)(2,1)}, u32[]{:S(2)}, u32[]{:S(2)}) collective-permute-start(bf16[2048,128]{1,0:T(8,128)(2,1)} %get-tuple-element.580), channel_id=1, source_target_pairs={{0,4},{4,0},{1,5},{5,1},{2,6},{6,2},{3,7},{7,3},{8,9},{12,13},{9,8... | collective-permute-start | bytes 1572872 | tf_op jit(solution)/shard_map/while/body/eval_jaxpr/cond/branch_13_fun/ppermute | solution.py:363
  98.8 44.5 %collective-permute-start.43 = (bf16[2048,128]{1,0:T(8,128)(2,1)S(1)}, bf16[2048,128]{1,0:T(8,128)(2,1)}, u32[]{:S(2)}, u32[]{:S(2)}) collective-permute-start(bf16[2048,128]{1,0:T(8,128)(2,1)S(1)} %broadcast_select_fusion.8), channel_id=1, source_target_pairs={{0,4},{4,0},{1,5},{5,1},{2,6},{6,2},{3,11},{7,15},{8,12},{12,8},{9... | collective-permute-start | bytes 1572872 | tf_op jit(solution)/shard_map/while/body/eval_jaxpr/cond/branch_13_fun/ppermute | solution.py:363
  141.6 2.4 collective-permute-start.44
  146.9 2.3 collective-permute-start.27
  151.0 47.3 %collective-permute-start.28 = (bf16[2048,128]{1,0:T(8,128)(2,1)S(1)}, bf16[2048,128]{1,0:T(8,128)(2,1)}, u32[]{:S(2)}, u32[]{:S(2)}) collective-permute-start(bf16[2048,128]{1,0:T(8,128)(2,1)S(1)} %broadcast_select_fusion.3), channel_id=1, source_target_pairs={{0,4},{4,0},{1,5},{5,1},{2,6},{6,2},{3,7},{7,3},{8,12},{12,8},{9,1... | collective-permute-start | bytes 1572872 | tf_op jit(solution)/shard_map/while/body/eval_jaxpr/cond/branch_6_fun/ppermute | solution.py:363
  151.4 48.6 %collective-permute-start.29 = (bf16[2048,128]{1,0:T(8,128)(2,1)S(1)}, bf16[2048,128]{1,0:T(8,128)(2,1)}, u32[]{:S(2)}, u32[]{:S(2)}) collective-permute-start(bf16[2048,128]{1,0:T(8,128)(2,1)S(1)} %branch_6_fun.1), channel_id=1, source_target_pairs={{0,4},{4,0},{1,9},{5,13},{2,6},{6,2},{3,7},{7,3},{8,12},{12,8},{9,... | collective-permute-start | bytes 1572872 | tf_op jit(solution)/shard_map/while/body/eval_jaxpr/cond/branch_6_fun/ppermute | solution.py:363
  203.8 34.6 %collective-permute-start.36 = (bf16[2048,128]{1,0:T(8,128)(2,1)}, bf16[2048,128]{1,0:T(8,128)(2,1)}, u32[]{:S(2)}, u32[]{:S(2)}) collective-permute-start(bf16[2048,128]{1,0:T(8,128)(2,1)} %get-tuple-element.548), channel_id=1, source_target_pairs={{0,4},{4,0},{1,5},{5,1},{2,6},{6,2},{3,7},{7,3},{8,9},{12,13},{9,8... | collective-permute-start | bytes 1572872 | tf_op jit(solution)/shard_map/while/body/eval_jaxpr/cond/branch_9_fun/ppermute | solution.py:363
  240.1 4.9 collective-permute-start.37
  243.4 2.4 collective-permute-start.38
  249.1 2.9 collective-permute-start.4
  256.6 103.8 %collective-permute-start = (bf16[2048,128]{1,0:T(8,128)(2,1)}, bf16[2048,128]{1,0:T(8,128)(2,1)}, u32[]{:S(2)}, u32[]{:S(2)}) collective-permute-start(bf16[2048,128]{1,0:T(8,128)(2,1)} %param), channel_id=1, source_target_pairs={{0,8},{4,12},{1,0},{5,4},{2,6},{6,2},{3,7},{7,3},{8,1},{12,5},{9,1... | collective-permute-start | bytes 1572872 | tf_op jit(solution)/shard_map/while/body/eval_jaxpr/cond/branch_0_fun/ppermute | solution.py:363
  325.8 34.6 %collective-permute-start.1 = (bf16[2048,128]{1,0:T(8,128)(2,1)}, bf16[2048,128]{1,0:T(8,128)(2,1)}, u32[]{:S(2)}, u32[]{:S(2)}) collective-permute-start(bf16[2048,128]{1,0:T(8,128)(2,1)} %param), channel_id=1, source_target_pairs={{0,16},{4,20},{1,5},{5,1},{2,0},{6,4},{3,7},{7,3},{8,12},{12,8},{9... | collective-permute-start | bytes 1572872 | tf_op jit(solution)/shard_map/while/body/eval_jaxpr/cond/branch_0_fun/ppermute | solution.py:363
  331.6 28.8 %collective-permute-start.2 = (bf16[2048,128]{1,0:T(8,128)(2,1)}, bf16[2048,128]{1,0:T(8,128)(2,1)}, u32[]{:S(2)}, u32[]{:S(2)}) collective-permute-start(bf16[2048,128]{1,0:T(8,128)(2,1)} %param), channel_id=1, source_target_pairs={{0,24},{4,28},{1,5},{5,1},{2,6},{6,2},{3,0},{7,4},{8,12},{12,8},{9... | collective-permute-start | bytes 1572872 | tf_op jit(solution)/shard_map/while/body/eval_jaxpr/cond/branch_0_fun/ppermute | solution.py:363
  374.1 6.6 %collective-permute-start.21 = (bf16[2048,128]{1,0:T(8,128)(2,1)}, bf16[2048,128]{1,0:T(8,128)(2,1)}, u32[]{:S(2)}, u32[]{:S(2)}) collective-permute-start(bf16[2048,128]{1,0:T(8,128)(2,1)} %get-tuple-element.480), channel_id=1, source_target_pairs={{0,16},{4,20},{1,5},{5,1},{2,6},{6,2},{3,7},{7,3},{8,12},{12,8},{9... | collective-permute-start | bytes 1572872 | tf_op jit(solution)/shard_map/while/body/eval_jaxpr/cond/branch_2_fun/ppermute | solution.py:363
  382.4 20.6 %collective-permute-start.22 = (bf16[2048,128]{1,0:T(8,128)(2,1)S(1)}, bf16[2048,128]{1,0:T(8,128)(2,1)}, u32[]{:S(2)}, u32[]{:S(2)}) collective-permute-start(bf16[2048,128]{1,0:T(8,128)(2,1)S(1)} %broadcast_select_fusion.1), channel_id=1, source_target_pairs={{0,4},{4,0},{1,5},{5,1},{2,6},{6,2},{3,7},{7,3},{8,12},{12,8},{9,1... | collective-permute-start | bytes 1572872 | tf_op jit(solution)/shard_map/while/body/eval_jaxpr/cond/branch_2_fun/ppermute | solution.py:363
  382.9 32.9 %collective-permute-start.23 = (bf16[2048,128]{1,0:T(8,128)(2,1)S(1)}, bf16[2048,128]{1,0:T(8,128)(2,1)}, u32[]{:S(2)}, u32[]{:S(2)}) collective-permute-start(bf16[2048,128]{1,0:T(8,128)(2,1)S(1)} %branch_2_fun.1), channel_id=1, source_target_pairs={{0,8},{4,12},{1,5},{5,1},{2,6},{6,2},{3,7},{7,3},{8,0},{12,4},{9,1... | collective-permute-start | bytes 1572872 | tf_op jit(solution)/shard_map/while/body/eval_jaxpr/cond/branch_2_fun/ppermute | solution.py:363
  429.5 16.0 %collective-permute-start.13 = (bf16[2048,128]{1,0:T(8,128)(2,1)}, bf16[2048,128]{1,0:T(8,128)(2,1)}, u32[]{:S(2)}, u32[]{:S(2)}) collective-permute-start(bf16[2048,128]{1,0:T(8,128)(2,1)} %get-tuple-element.550), channel_id=1, source_target_pairs={{0,4},{4,0},{1,5},{5,1},{2,6},{6,2},{3,7},{7,3},{8,12},{12,8},{9,1... | collective-permute-start | bytes 1572872 | tf_op jit(solution)/shard_map/while/body/eval_jaxpr/cond/branch_11_fun/ppermute | solution.py:363
  432.4 14.8 %collective-permute-start.14 = (bf16[2048,128]{1,0:T(8,128)(2,1)S(1)}, bf16[2048,128]{1,0:T(8,128)(2,1)}, u32[]{:S(2)}, u32[]{:S(2)}) collective-permute-start(bf16[2048,128]{1,0:T(8,128)(2,1)S(1)} %branch_11_fun.1), channel_id=1, source_target_pairs={{0,4},{4,0},{1,5},{5,1},{2,18},{6,22},{3,7},{7,3},{8,12},{12,8},{9... | collective-permute-start | bytes 1572872 | tf_op jit(solution)/shard_map/while/body/eval_jaxpr/cond/branch_11_fun/ppermute | solution.py:363
  450.1 30.7 %collective-permute-start.15 = (bf16[2048,128]{1,0:T(8,128)(2,1)}, bf16[2048,128]{1,0:T(8,128)(2,1)}, u32[]{:S(2)}, u32[]{:S(2)}) collective-permute-start(bf16[2048,128]{1,0:T(8,128)(2,1)} %param.15), channel_id=1, source_target_pairs={{0,4},{4,0},{1,5},{5,1},{2,6},{6,2},{3,24},{7,28},{8,12},{12,8},{9... | collective-permute-start | bytes 1572872 | tf_op jit(solution)/shard_map/while/body/eval_jaxpr/cond/branch_15_fun/ppermute | solution.py:363
  478.9 2.6 collective-permute-start.16
  479.0 3.2 collective-permute-start.17
  482.9 3.1 collective-permute-start.53
  487.4 63.0 %all-to-all-start = ((f32[4,2,512,128]{3,2,1,0:T(8,128)}), f32[4,2,512,128]{3,2,1,0:T(8,128)S(1)}, u32[]{:S(2)}, u32[]{:S(2)}) async-start(f32[4,2,512,128]{3,2,1,0:T(8,128)} %copy.21), calls=%async_computation | async-start | bytes 4194304 | tf_op jit(solution)/shard_map/all_to_all | solution.py:452
  568.9 9.0 %collective-permute-start.54 = (bf16[2048,128]{1,0:T(8,128)(2,1)S(1)}, bf16[2048,128]{1,0:T(8,128)(2,1)S(1)}, u32[]{:S(2)}, u32[]{:S(2)}) collective-permute-start(bf16[2048,128]{1,0:T(8,128)(2,1)S(1)} %bitcast.55), channel_id=1, source_target_pairs={{0,4},{1,5},{2,6},{3,7},{4,0},{5,1},{6,2},{7,3},{8,12},{9,13},{10,... | collective-permute-start | bytes 1572872 | tf_op jit(solution)/shard_map/ppermute | solution.py:363
  (12 other events, 106.9 us)

commit v3 on v2

--- a/solution.py
+++ b/solution.py
@@ -44,7 +44,7 @@
     out_ref[...] = jnp.broadcast_to(jnp.sum(kept, axis=1, keepdims=True), out_ref.shape).astype(out_ref.dtype)
 
 
-def diagonal(gram, core, fine=128):
+def diagonal(gram, core, lanes, fine=512):
     width = gram.shape[0]
     tiles = width // fine
     return pl.pallas_call(
@@ -53,9 +53,9 @@
             num_scalar_prefetch=1,
             grid=(tiles,),
             in_specs=[pl.BlockSpec((fine, fine), lambda i, s: (i, s[0] * tiles + i))],
-            out_specs=pl.BlockSpec((fine, fine), lambda i, s: (i, 0)),
-        ),
-        out_shape=jax.ShapeDtypeStruct((width, fine), gram.dtype),
+            out_specs=pl.BlockSpec((fine, lanes), lambda i, s: (i, 0)),
+        ),
+        out_shape=jax.ShapeDtypeStruct((width, lanes), gram.dtype),
         compiler_params=pltpu.CompilerParams(dimension_semantics=("arbitrary",)),
     )(core.reshape(1), gram)
 
@@ -176,7 +176,7 @@
     lax.fori_loop(0, count, body, 0)
 
 
-def relay_kernel(t_ref, s_ref, x, step, g_own, g_sib, acc, send, x_v, acc_v, out_v, tiles_v, sems, tile_sems):
+def relay_kernel(t_ref, s_ref, x, step, pay, g_own, g_sib, acc, send, late, x_v, acc_v, out_v, tiles_v, sems, tile_sems):
     field = lambda name: at(t_ref, s_ref, name)
 
     @pl.when(field(RELAYS) == 1)
@@ -190,38 +190,44 @@
         def store(part, change):
             out_v[part] = (acc_v[part] + change).astype(jnp.bfloat16)
 
+        onward = fetch(x_v, late, sems.at[4])
         add_block(own, g_own, g_sib, slot, x_v, tiles_v, tile_sems, store)
         fetch(out_v, send, sems.at[2]).wait()
+        onward.wait()
 
     @pl.when((field(RELAYS) == 0) & (field(VISITED) == 1))
     def _():
         fetch(step, send, sems.at[3]).wait()
 
-
-def relay(turn, table, x, step, g_own, g_sib, acc, tile=1024):
+    @pl.when((field(RELAYS) == 0) & ((field(VISITED) == 1) | (field(SENDS) == 1)))
+    def _():
+        fetch(pay, late, sems.at[4]).wait()
+
+
+def relay(turn, table, x, step, pay, g_own, g_sib, acc, tile=1024):
     width, resp = x.shape
     anywhere = pl.BlockSpec(memory_space=pl.ANY)
     return pl.pallas_call(
         relay_kernel,
         grid_spec=pltpu.PrefetchScalarGridSpec(
             num_scalar_prefetch=2,
-            in_specs=[anywhere] * 5,
-            out_specs=anywhere,
+            in_specs=[anywhere] * 6,
+            out_specs=[anywhere, anywhere],
             scratch_shapes=[
                 pltpu.VMEM((width, resp), jnp.bfloat16),
                 pltpu.VMEM((width, resp), jnp.float32),
                 pltpu.VMEM((width, resp), jnp.bfloat16),
                 pltpu.VMEM((2, tile, width), jnp.bfloat16),
-                pltpu.SemaphoreType.DMA((4,)),
+                pltpu.SemaphoreType.DMA((5,)),
                 pltpu.SemaphoreType.DMA((2,)),
             ],
         ),
-        out_shape=jax.ShapeDtypeStruct((width, resp), jnp.bfloat16),
+        out_shape=[jax.ShapeDtypeStruct((width, resp), jnp.bfloat16)] * 2,
         compiler_params=pltpu.CompilerParams(vmem_limit_bytes=16 << 20),
         cost_estimate=pl.CostEstimate(
             flops=2 * resp * width * width, bytes_accessed=2 * width * width, transcendentals=0
         ),
-    )(turn, table, x, step, g_own, g_sib, acc)
+    )(turn, table, x, step, pay, g_own, g_sib, acc)
 
 
 def update_kernel(t_ref, s_ref, g_own, g_sib, acc_in, moved_in, *rest):
@@ -339,7 +345,7 @@
 
 
 def routes(p, pn, planes, lines):
-    rest_q = [c for c in range(lines) if c not in (p, pn)]
+    rest_q = sorted([c for c in range(lines) if c not in (p, pn)], key=lambda c: c == pn ^ 1)
     rest_z = sorted([c for c in range(planes) if c not in (p, pn)], key=lambda c: abs(c - p) - abs(c - pn))
     if p == pn:
         return [([((p, p), (c, p)), ((p, c), (p, p))], c, p) for c in rest_z]
@@ -392,12 +398,10 @@
             for n, (_, plane, _) in enumerate(routes(p, pn, planes, lines)):
                 holds[p, pn, plane] = n + 1
             holds[p, pn, p] = 0
-    after = jnp.concatenate([order, order[-1:]])
-    order = jnp.concatenate([order[:1], order])
-    real = flag(jnp.arange(order.shape[0]) > 0)
+    after = jnp.concatenate([order[1:], order[-1:]])
     pair, pair_n, slot_n = order // 2, after // 2, after % 2
     held = lax.dynamic_index_in_dim(jnp.asarray(holds), z, 2, keepdims=False)[pair, pair_n]
-    line = flag(q == pair) * real
+    line = flag(q == pair)
     table = jnp.stack(
         [
             order % 2,
@@ -422,14 +426,11 @@
             turn, step, pay, acc = operands
             if p == pn:
                 return tuple(send(pay, flows) for flows, _, _ in plan)
-            at_pn = (z == pn) & (q == p)
             first = send(pay, plan[0][0])
-            out = relay(turn, table, first, step, gram, g_sib, acc)
-            late, late_pay, out = lax.optimization_barrier((first, pay, out))
-            between = [
-                send(pay if source == p else jnp.where(at_pn, late, late_pay), flows) for flows, _, source in plan[1:-1]
-            ]
-            return (first, *between, send(out, plan[-1][0]))
+            out, late = relay(turn, table, first, step, pay, gram, g_sib, acc)
+            last = send(out, plan[-1][0])
+            between = [send(pay if source == p else late, flows) for flows, _, source in plan[1:-1]]
+            return (first, *between, last)
 
         return run
 
@@ -444,7 +445,17 @@
         return acc, moved, got
 
     empty = jnp.zeros((2, width, half), jnp.bfloat16)
-    carry = (shares, empty, (empty[0],) * (planes - 1))
+
+    def opening(p):
+        def run(payload):
+            return tuple(
+                permute(payload, device_pairs([((p, c), (p, p))], planes, lines)) for c in range(lines) if c != p
+            )
+
+        return run
+
+    began = lax.dynamic_index_in_dim(shares, (order[0] % 2) ^ k, 0, keepdims=False).astype(jnp.bfloat16)
+    carry = (shares, empty, lax.switch(order[0] // 2, [opening(p) for p in range(planes)], began))
     acc, moved, _ = lax.fori_loop(0, order.shape[0], visit, carry)
 
     part = width // lines
@@ -453,6 +464,7 @@
     beta = join(
         core, moved.reshape(2 * width, half), moved_other.reshape(2 * width, half), (beta_start,)
     )
+    share, beta = lax.optimization_barrier((share, beta))
     share = lax.dynamic_slice_in_dim(corr, q * part, part, 1) - jnp.sum(share, axis=0)
     final = gather_col(share.astype(jnp.bfloat16))
     other = permute(final[:, 1].reshape(width, half), swap)

time: 587 us -> 582 us (level)
  starting transfers between devices: 315 us -> 325 us
  Pallas kernels: 71.9 us -> 64.9 us
  waiting for transfers between devices: 111 us -> 104 us
    ppermute x34, starting transfers between devices: 277 us -> 295 us  [per_device(): permute = lambda x, pairs: lax.ppermute(x, ('row', 'col'), pairs)]
    all_to_all x1, waiting for transfers between devices: 25.2 us -> 16.3 us  [per_device(): lax.all_to_all(acc.reshape(2, lines, part, half).swapaxes(0, 1), 'col', 0...]
    all_to_all x1, starting transfers between devices: 37.8 us -> 29.9 us  [per_device(): lax.all_to_all(acc.reshape(2, lines, part, half).swapaxes(0, 1), 'col', 0...]
    pallas_call x9 -> x8, Pallas kernels: 27.2 us -> 26.3 us  [update(): pl.pallas_call(update_kernel, grid_spec=pltpu.PrefetchScalarGridSpec(num_...]
  transfers between devices with their start and end apart: 35 -> 35, of which waited for: 23 -> 22; matrix products, arithmetic and copies ran while one was open for 7% -> 7% of each run, Pallas kernels for 5% -> 4%
where the time goes in v3:
time: 582 us; the launch traced here: 574 us
  starting transfers between devices  325 us (56%)
  waiting for transfers between devices  104 us (18%)
  Pallas kernels  64.9 us (11%)
  local copies, waits for them, and re-layouts  26.9 us (5%)
  blocking collectives  16.1 us (3%)
  other arithmetic  15 us (3%)
  matrix products  12.3 us (2%)
  loops' own time  6.07 us (1%)
    ppermute x34, starting transfers between devices, per_device(): permute = lambda x, pairs: lax.ppermute(x, ('row', 'col'), pairs)  295 us
    ppermute x34, waiting for transfers between devices, per_device(): permute = lambda x, pairs: lax.ppermute(x, ('row', 'col'), pairs)  88 us
    all_to_all x1, starting transfers between devices, per_device(): lax.all_to_all(acc.reshape(2, lines, part, half).swapaxes(0, 1), 'col', 0...  29.9 us
    pallas_call x8, Pallas kernels, update(): pl.pallas_call(update_kernel, grid_spec=pltpu.PrefetchScalarGridSpec(num_...  26.3 us
    all_to_all x1, waiting for transfers between devices, per_device(): lax.all_to_all(acc.reshape(2, lines, part, half).swapaxes(0, 1), 'col', 0...  16.3 us
    all_to_all x1, blocking collectives, gather_col(): lax.all_to_all(jnp.broadcast_to(x[None], (lines, *x.shape)), 'col', 0, 0)  16.1 us
    pallas_call x2, Pallas kernels, join(): pl.pallas_call(join_kernel, grid_spec=pltpu.PrefetchScalarGridSpec(num_sc...  13.1 us
    dot_general x1, matrix products, per_device(): product = jnp.dot(gram, flat, preferred_element_type=jnp.float32)  12.3 us
  transfers between devices with their start and end apart: 35, of which 22 were waited for; matrix products, arithmetic and copies ran while one was open for 7% of the time, Pallas kernels for 4%

profile of v3, /device:TPU:8, one launch (start us, length us, event | category | flops | bytes accessed | tf_op | source)
XLA Modules:
  0.0 573.8 jit_solution(7551400066792366758)
XLA Ops:
  0.8 8.8 %shard_map.104 = (f32[4096,128]{1,0:T(8,128)}, bf16[4096,256]{1,0:T(8,128)(2,1)}) custom-call(s32[1]{0:T(128)} %bitcast.2.k_ref.s_ref, f32[4096,2,128]{2,1,0:T(2,128)} %rest_0_.1), custom_call_target="tpu_custom_call" | custom-call | tf_op jit(solution)/shard_map/pallas_call | solution.py:308
  9.5 12.3 %fusion.24 = f32[256,2048]{1,0:T(8,128)} fusion(bf16[4096,256]{1,0:T(8,128)(2,1)} %get-tuple-element.537, bf16[2048,4096]{1,0:T(8,128)(2,1)} %block_ref.1), kind=kOutput, calls=%fused_computation.76 | convolution fusion | flops 4294967296 | bytes 20971520 | tf_op jit(solution)/shard_map/dot_general | solution.py:379
  32.2 7.6 %gather_fusion.1 = f32[2048,128]{1,0:T(8,128)} fusion(f32[2048,128]{1,0:T(8,128)S(1)} %bitcast.66, s32[2048]{0:T(1024)S(1)} %get-tuple-element.656), kind=kCustom, calls=%fused_computation.1 | custom fusion | bytes 2105344 | tf_op jit(solution)/shard_map/gather | solution.py:384
  63.7 423.8 %while.21 = (s32[]{:T(128)}, f32[2,2048,128]{2,1,0:T(8,128)S(1)}, bf16[2,2048,128]{2,1,0:T(8,128)(2,1)S(1)}, bf16[2048,128]{1,0:T(8,128)(2,1)}, bf16[2048,128]{1...) while((s32[]{:T(128)}, f32[2,2048,128]{2,1,0:T(8,128)S(1)}, ...), condition=%wide.region_22.23_spmd, body=%wide.region_5.22_spmd.sunk | while | flops 3226468352 | bytes 38273432 | solution.py:459
  74.5 107.9 %conditional.4 = (bf16[2048,128]{1,0:T(8,128)(2,1)}, bf16[2048,128]{1,0:T(8,128)(2,1)}, bf16[2048,128]{1,0:T(8,128)(2,1)}) conditional(s32[]{:T(128)} %bitcast.65, bf16[2048,128]{1,0:T(8,128)(2,1)S(1)} %get-tuple-element.770, (bf16[2048,128]{1,0:T(8,128)(2,1)S(1)}, s32[1]{0:T(128)}, s32[72]{0:T(128)S(1)}, ...), branch_computations={%region_6.6_spmd, %region_7.7_spmd, %region_8.8_spmd, %region_9.9_... | conditional | flops 1073741824 | bytes 14680208 | solution.py:443
  74.6 68.0 %collective-permute-start.18 = (bf16[2048,128]{1,0:T(8,128)(2,1)S(1)}, bf16[2048,128]{1,0:T(8,128)(2,1)}, u32[]{:S(2)}, u32[]{:S(2)}) collective-permute-start(bf16[2048,128]{1,0:T(8,128)(2,1)S(1)} %get-tuple-element.403.pay), channel_id=1, source_target_pairs={{0,16},{4,20},{1,5},{5,1},{2,6},{6,2},{3,7},{7,3},{8,12},{12,8},{9... | collective-permute-start | bytes 1572872 | tf_op jit(solution)/shard_map/while/body/eval_jaxpr/cond/branch_2_fun/ppermute | solution.py:369
  144.9 19.1 %collective-permute-start.19 = (bf16[2048,128]{1,0:T(8,128)(2,1)S(1)}, bf16[2048,128]{1,0:T(8,128)(2,1)}, u32[]{:S(2)}, u32[]{:S(2)}) collective-permute-start(bf16[2048,128]{1,0:T(8,128)(2,1)S(1)} %get-tuple-element.410), channel_id=1, source_target_pairs={{0,4},{4,0},{1,5},{5,1},{2,6},{6,2},{3,7},{7,3},{8,12},{12,8},{9,1... | collective-permute-start | bytes 1572872 | tf_op jit(solution)/shard_map/while/body/eval_jaxpr/cond/branch_2_fun/ppermute | solution.py:369
  169.8 12.7 %collective-permute-done.20 = bf16[2048,128]{1,0:T(8,128)(2,1)} collective-permute-done((bf16[2048,128]{1,0:T(8,128)(2,1)S(1)}, bf16[2048,128]{1,0:T(8,128)(2,1)}, u32[]{:S(2)}, u32[]{:S(2)}) %collective-permute-start.20) | collective-permute-done | bytes 524320 | tf_op jit(solution)/shard_map/while/body/eval_jaxpr/cond/branch_2_fun/ppermute | solution.py:369
  182.5 11.3 %eval_jaxpr.11 = (f32[2,2048,128]{2,1,0:T(8,128)S(1)}, bf16[2,2048,128]{2,1,0:T(8,128)(2,1)S(1)}) custom-call(s32[1]{0:T(128)} %bitcast.64.t_ref, s32[72]{0:T(128)S(1)} %get-tuple-element.880.s_ref, bf16[2048,4096]{1,0:T(8,128)(2,1)} %get-tuple-element.888.g_own, ...), custom_call_target="tpu_custom_call", output_to_operand_aliasing={{0}: (4, {}), {1}: (5, {})} | custom-call | flops 2147483648 | bytes 16777216 | tf_op jit(solution)/shard_map/while/body/eval_jaxpr/pallas_call | solution.py:271
  196.8 28.5 %conditional.4 = (bf16[2048,128]{1,0:T(8,128)(2,1)}, bf16[2048,128]{1,0:T(8,128)(2,1)}, bf16[2048,128]{1,0:T(8,128)(2,1)}) conditional(s32[]{:T(128)} %bitcast.65, bf16[2048,128]{1,0:T(8,128)(2,1)S(1)} %get-tuple-element.770, (bf16[2048,128]{1,0:T(8,128)(2,1)S(1)}, s32[1]{0:T(128)}, s32[72]{0:T(128)S(1)}, ...), branch_computations={%region_6.6_spmd, %region_7.7_spmd, %region_8.8_spmd, %region_9.9_... | conditional | flops 1073741824 | bytes 14680208 | solution.py:443
  199.7 11.4 %collective-permute-start.40 = (bf16[2048,128]{1,0:T(8,128)(2,1)S(1)}, bf16[2048,128]{1,0:T(8,128)(2,1)}, u32[]{:S(2)}, u32[]{:S(2)}) collective-permute-start(bf16[2048,128]{1,0:T(8,128)(2,1)S(1)} %get-tuple-element.463), channel_id=1, source_target_pairs={{0,4},{4,0},{1,5},{5,1},{2,10},{6,14},{3,7},{7,3},{8,9},{12,13},{9... | collective-permute-start | bytes 1572872 | tf_op jit(solution)/shard_map/while/body/eval_jaxpr/cond/branch_9_fun/ppermute | solution.py:369
  211.2 14.1 %collective-permute-done.40 = bf16[2048,128]{1,0:T(8,128)(2,1)} collective-permute-done((bf16[2048,128]{1,0:T(8,128)(2,1)S(1)}, bf16[2048,128]{1,0:T(8,128)(2,1)}, u32[]{:S(2)}, u32[]{:S(2)}) %collective-permute-start.40) | collective-permute-done | bytes 524320 | tf_op jit(solution)/shard_map/while/body/eval_jaxpr/cond/branch_9_fun/ppermute | solution.py:369
  229.0 59.2 %conditional.4 = (bf16[2048,128]{1,0:T(8,128)(2,1)}, bf16[2048,128]{1,0:T(8,128)(2,1)}, bf16[2048,128]{1,0:T(8,128)(2,1)}) conditional(s32[]{:T(128)} %bitcast.65, bf16[2048,128]{1,0:T(8,128)(2,1)S(1)} %get-tuple-element.770, (bf16[2048,128]{1,0:T(8,128)(2,1)S(1)}, s32[1]{0:T(128)}, s32[72]{0:T(128)S(1)}, ...), branch_computations={%region_6.6_spmd, %region_7.7_spmd, %region_8.8_spmd, %region_9.9_... | conditional | flops 1073741824 | bytes 14680208 | solution.py:443
  229.1 24.4 %collective-permute-start.29 = (bf16[2048,128]{1,0:T(8,128)(2,1)S(1)}, bf16[2048,128]{1,0:T(8,128)(2,1)}, u32[]{:S(2)}, u32[]{:S(2)}) collective-permute-start(bf16[2048,128]{1,0:T(8,128)(2,1)S(1)} %param.9), channel_id=1, source_target_pairs={{0,4},{4,0},{1,5},{5,1},{2,6},{6,2},{3,7},{7,3},{8,12},{12,8},{9,2... | collective-permute-start | bytes 1572872 | tf_op jit(solution)/shard_map/while/body/eval_jaxpr/cond/branch_5_fun/ppermute | solution.py:369
  253.5 5.7 collective-permute-start.28
  259.2 5.7 collective-permute-start.27
  265.0 23.3 %collective-permute-done.27 = bf16[2048,128]{1,0:T(8,128)(2,1)} collective-permute-done((bf16[2048,128]{1,0:T(8,128)(2,1)S(1)}, bf16[2048,128]{1,0:T(8,128)(2,1)}, u32[]{:S(2)}, u32[]{:S(2)}) %collective-permute-start.27) | collective-permute-done | bytes 524320 | tf_op jit(solution)/shard_map/while/body/eval_jaxpr/cond/branch_5_fun/ppermute | solution.py:369
  291.1 39.1 %conditional.4 = (bf16[2048,128]{1,0:T(8,128)(2,1)}, bf16[2048,128]{1,0:T(8,128)(2,1)}, bf16[2048,128]{1,0:T(8,128)(2,1)}) conditional(s32[]{:T(128)} %bitcast.65, bf16[2048,128]{1,0:T(8,128)(2,1)S(1)} %get-tuple-element.770, (bf16[2048,128]{1,0:T(8,128)(2,1)S(1)}, s32[1]{0:T(128)}, s32[72]{0:T(128)S(1)}, ...), branch_computations={%region_6.6_spmd, %region_7.7_spmd, %region_8.8_spmd, %region_9.9_... | conditional | flops 1073741824 | bytes 14680208 | solution.py:443
  291.1 13.3 %collective-permute-start.33 = (bf16[2048,128]{1,0:T(8,128)(2,1)S(1)}, bf16[2048,128]{1,0:T(8,128)(2,1)}, u32[]{:S(2)}, u32[]{:S(2)}) collective-permute-start(bf16[2048,128]{1,0:T(8,128)(2,1)S(1)} %get-tuple-element.438.pay), channel_id=1, source_target_pairs={{0,4},{4,0},{1,5},{5,1},{2,6},{6,2},{3,7},{7,3},{8,12},{12,8},{9,2... | collective-permute-start | bytes 1572872 | tf_op jit(solution)/shard_map/while/body/eval_jaxpr/cond/branch_7_fun/ppermute | solution.py:369
  307.2 21.3 %collective-permute-start.35 = (bf16[2048,128]{1,0:T(8,128)(2,1)S(1)}, bf16[2048,128]{1,0:T(8,128)(2,1)}, u32[]{:S(2)}, u32[]{:S(2)}) collective-permute-start(bf16[2048,128]{1,0:T(8,128)(2,1)S(1)} %get-tuple-element.446), channel_id=1, source_target_pairs={{0,4},{4,0},{1,9},{5,13},{2,6},{6,2},{3,7},{7,3},{8,12},{12,8},{9,... | collective-permute-start | bytes 1572872 | tf_op jit(solution)/shard_map/while/body/eval_jaxpr/cond/branch_7_fun/ppermute | solution.py:369
  341.4 100.7 %conditional.4 = (bf16[2048,128]{1,0:T(8,128)(2,1)}, bf16[2048,128]{1,0:T(8,128)(2,1)}, bf16[2048,128]{1,0:T(8,128)(2,1)}) conditional(s32[]{:T(128)} %bitcast.65, bf16[2048,128]{1,0:T(8,128)(2,1)S(1)} %get-tuple-element.770, (bf16[2048,128]{1,0:T(8,128)(2,1)S(1)}, s32[1]{0:T(128)}, s32[72]{0:T(128)S(1)}, ...), branch_computations={%region_6.6_spmd, %region_7.7_spmd, %region_8.8_spmd, %region_9.9_... | conditional | flops 1073741824 | bytes 14680208 | solution.py:443
  341.5 59.9 %collective-permute-start.21 = (bf16[2048,128]{1,0:T(8,128)(2,1)S(1)}, bf16[2048,128]{1,0:T(8,128)(2,1)}, u32[]{:S(2)}, u32[]{:S(2)}) collective-permute-start(bf16[2048,128]{1,0:T(8,128)(2,1)S(1)} %get-tuple-element.412.pay), channel_id=1, source_target_pairs={{0,24},{4,28},{1,5},{5,1},{2,6},{6,2},{3,7},{7,3},{8,12},{12,8},{9... | collective-permute-start | bytes 1572872 | tf_op jit(solution)/shard_map/while/body/eval_jaxpr/cond/branch_3_fun/ppermute | solution.py:369
  403.7 20.0 %collective-permute-start.22 = (bf16[2048,128]{1,0:T(8,128)(2,1)S(1)}, bf16[2048,128]{1,0:T(8,128)(2,1)}, u32[]{:S(2)}, u32[]{:S(2)}) collective-permute-start(bf16[2048,128]{1,0:T(8,128)(2,1)S(1)} %get-tuple-element.419), channel_id=1, source_target_pairs={{0,4},{4,0},{1,5},{5,1},{2,6},{6,2},{3,7},{7,3},{8,12},{12,8},{9,1... | collective-permute-start | bytes 1572872 | tf_op jit(solution)/shard_map/while/body/eval_jaxpr/cond/branch_3_fun/ppermute | solution.py:369
  423.7 5.7 collective-permute-start.23
  429.4 12.7 %collective-permute-done.23 = bf16[2048,128]{1,0:T(8,128)(2,1)} collective-permute-done((bf16[2048,128]{1,0:T(8,128)(2,1)S(1)}, bf16[2048,128]{1,0:T(8,128)(2,1)}, u32[]{:S(2)}, u32[]{:S(2)}) %collective-permute-start.23) | collective-permute-done | bytes 524320 | tf_op jit(solution)/shard_map/while/body/eval_jaxpr/cond/branch_3_fun/ppermute | solution.py:369
  442.1 11.3 %eval_jaxpr.11 = (f32[2,2048,128]{2,1,0:T(8,128)S(1)}, bf16[2,2048,128]{2,1,0:T(8,128)(2,1)S(1)}) custom-call(s32[1]{0:T(128)} %bitcast.64.t_ref, s32[72]{0:T(128)S(1)} %get-tuple-element.880.s_ref, bf16[2048,4096]{1,0:T(8,128)(2,1)} %get-tuple-element.888.g_own, ...), custom_call_target="tpu_custom_call", output_to_operand_aliasing={{0}: (4, {}), {1}: (5, {})} | custom-call | flops 2147483648 | bytes 16777216 | tf_op jit(solution)/shard_map/while/body/eval_jaxpr/pallas_call | solution.py:271
  455.7 31.2 %conditional.4 = (bf16[2048,128]{1,0:T(8,128)(2,1)}, bf16[2048,128]{1,0:T(8,128)(2,1)}, bf16[2048,128]{1,0:T(8,128)(2,1)}) conditional(s32[]{:T(128)} %bitcast.65, bf16[2048,128]{1,0:T(8,128)(2,1)S(1)} %get-tuple-element.770, (bf16[2048,128]{1,0:T(8,128)(2,1)S(1)}, s32[1]{0:T(128)}, s32[72]{0:T(128)S(1)}, ...), branch_computations={%region_6.6_spmd, %region_7.7_spmd, %region_8.8_spmd, %region_9.9_... | conditional | flops 1073741824 | bytes 14680208 | solution.py:443
  455.8 23.7 %collective-permute-start.58 = (bf16[2048,128]{1,0:T(8,128)(2,1)S(1)}, bf16[2048,128]{1,0:T(8,128)(2,1)}, u32[]{:S(2)}, u32[]{:S(2)}) collective-permute-start(bf16[2048,128]{1,0:T(8,128)(2,1)S(1)} %param.19), channel_id=1, source_target_pairs={{0,4},{4,0},{1,5},{5,1},{2,6},{6,2},{3,7},{7,3},{8,12},{12,8},{9,1... | collective-permute-start | bytes 1572872 | tf_op jit(solution)/shard_map/while/body/eval_jaxpr/cond/branch_15_fun/ppermute | solution.py:369
  492.6 29.9 %all-to-all-start = ((f32[4,2,512,128]{3,2,1,0:T(8,128)}), f32[4,2,512,128]{3,2,1,0:T(8,128)S(1)}, u32[]{:S(2)}, u32[]{:S(2)}) async-start(f32[4,2,512,128]{3,2,1,0:T(8,128)} %copy.37), calls=%async_computation | async-start | bytes 4194304 | tf_op jit(solution)/shard_map/all_to_all | solution.py:463
  522.6 8.9 %shard_map.106 = f32[4096,2,128]{2,1,0:T(2,128)} custom-call(s32[1]{0:T(128)} %bitcast.2.k_ref.s_ref, bf16[4096,128]{1,0:T(8,128)(2,1)S(1)} %bitcast.69, bf16[4096,128]{1,0:T(8,128)(2,1)} %bitcast.76, f32[4096,2,128]{2,1,0:T(2,128)} %rest_0_.1), custom_call_target="tpu_custom_call" | custom-call | flops 2097152 | bytes 10485760 | tf_op jit(solution)/shard_map/pallas_call | solution.py:337
  531.4 16.3 %all-to-all-done = f32[4,2,512,128]{3,2,1,0:T(8,128)S(1)} async-done(((f32[4,2,512,128]{3,2,1,0:T(8,128)}), f32[4,2,512,128]{3,2,1,0:T(8,128)S(1)}, u32[]{:S(2)}, u32[]{:S(2)}) %all-to-all-start) | async-done | bytes 2097184 | tf_op jit(solution)/shard_map/all_to_all | solution.py:463
  550.0 16.1 %all_to_all.10 = bf16[4,2,512,128]{3,2,1,0:T(8,128)(2,1)S(1)} all-to-all(bf16[4,2,512,128]{3,2,1,0:T(8,128)(2,1)S(1)} %broadcast_in_dim.48), channel_id=1, replica_groups=mesh['row'=8,'col'=4] {'col'}, dimensions={0} | all-to-all | bytes 2097152 | tf_op jit(solution)/shard_map/all_to_all | solution.py:374
  (145 shorter events, 116.0 us)
Async XLA Ops:
  0.6 62.9 %collective-permute-start.64 = (bf16[2048,4096]{1,0:T(8,128)(2,1)}, bf16[2048,4096]{1,0:T(8,128)(2,1)}, u32[]{:S(2)}, u32[]{:S(2)}) collective-permute-start(bf16[2048,4096]{1,0:T(8,128)(2,1)} %block_ref.1), channel_id=1, source_target_pairs={{0,4},{1,5},{2,6},{3,7},{4,0},{5,1},{6,2},{7,3},{8,12},{9,13},{10,... | collective-permute-start | bytes 50331656 | tf_op jit(solution)/shard_map/ppermute | solution.py:369
  24.5 17.1 %collective-permute-start.60 = (f32[2048,128]{0,1:T(8,128)}, f32[2048,128]{0,1:T(8,128)S(1)}, u32[]{:S(2)}, u32[]{:S(2)}) collective-permute-start(f32[2048,128]{0,1:T(8,128)} %get-tuple-element.652), channel_id=1, source_target_pairs={{0,4},{1,5},{2,6},{3,7},{4,0},{5,1},{6,2},{7,3},{8,12},{9,13},{10,... | collective-permute-start | bytes 3145736 | tf_op jit(solution)/shard_map/ppermute | solution.py:369
  28.6 23.3 %collective-permute-start.62 = (bf16[2048,128]{1,0:T(8,128)(2,1)}, bf16[2048,128]{1,0:T(8,128)(2,1)}, u32[]{:S(2)}, u32[]{:S(2)}) collective-permute-start(bf16[2048,128]{1,0:T(8,128)(2,1)} %shard_map.105), channel_id=1, source_target_pairs={{0,4},{1,5},{2,6},{3,7},{4,0},{5,1},{6,2},{7,3},{8,12},{9,13},{10,... | collective-permute-start | bytes 1572872 | tf_op jit(solution)/shard_map/ppermute | solution.py:369
  43.1 2.1 collective-permute-start.8
  43.6 2.4 collective-permute-start.7
  43.7 3.0 collective-permute-start.6
  48.1 9.6 %collective-permute-start.61 = (f32[2048,128]{1,0:T(8,128)}, f32[2048,128]{1,0:T(8,128)}, u32[]{:S(2)}, u32[]{:S(2)}) collective-permute-start(f32[2048,128]{1,0:T(8,128)} %broadcast_in_dim.47), channel_id=1, source_target_pairs={{0,4},{1,5},{2,6},{3,7},{4,0},{5,1},{6,2},{7,3},{8,12},{9,13},{10,... | collective-permute-start | bytes 3145736 | tf_op jit(solution)/shard_map/ppermute | solution.py:369
  48.4 12.4 %collective-permute-start.63 = (f32[2048,128]{1,0:T(8,128)S(1)}, f32[2048,128]{1,0:T(8,128)}, u32[]{:S(2)}, u32[]{:S(2)}) collective-permute-start(f32[2048,128]{1,0:T(8,128)S(1)} %copy-done.2), channel_id=1, source_target_pairs={{0,4},{1,5},{2,6},{3,7},{4,0},{5,1},{6,2},{7,3},{8,12},{9,13},{10,... | collective-permute-start | bytes 3145736 | tf_op jit(solution)/shard_map/ppermute | solution.py:369
  68.9 2.1 collective-permute-start.37
  69.3 2.4 collective-permute-start.38
  74.6 69.7 %collective-permute-start.18 = (bf16[2048,128]{1,0:T(8,128)(2,1)S(1)}, bf16[2048,128]{1,0:T(8,128)(2,1)}, u32[]{:S(2)}, u32[]{:S(2)}) collective-permute-start(bf16[2048,128]{1,0:T(8,128)(2,1)S(1)} %get-tuple-element.403.pay), channel_id=1, source_target_pairs={{0,16},{4,20},{1,5},{5,1},{2,6},{6,2},{3,7},{7,3},{8,12},{12,8},{9... | collective-permute-start | bytes 1572872 | tf_op jit(solution)/shard_map/while/body/eval_jaxpr/cond/branch_2_fun/ppermute | solution.py:369
  144.9 24.9 %collective-permute-start.19 = (bf16[2048,128]{1,0:T(8,128)(2,1)S(1)}, bf16[2048,128]{1,0:T(8,128)(2,1)}, u32[]{:S(2)}, u32[]{:S(2)}) collective-permute-start(bf16[2048,128]{1,0:T(8,128)(2,1)S(1)} %get-tuple-element.410), channel_id=1, source_target_pairs={{0,4},{4,0},{1,5},{5,1},{2,6},{6,2},{3,7},{7,3},{8,12},{12,8},{9,1... | collective-permute-start | bytes 1572872 | tf_op jit(solution)/shard_map/while/body/eval_jaxpr/cond/branch_2_fun/ppermute | solution.py:369
  164.0 18.4 %collective-permute-start.20 = (bf16[2048,128]{1,0:T(8,128)(2,1)S(1)}, bf16[2048,128]{1,0:T(8,128)(2,1)}, u32[]{:S(2)}, u32[]{:S(2)}) collective-permute-start(bf16[2048,128]{1,0:T(8,128)(2,1)S(1)} %get-tuple-element.411), channel_id=1, source_target_pairs={{0,8},{4,12},{1,5},{5,1},{2,6},{6,2},{3,7},{7,3},{8,0},{12,4},{9,1... | collective-permute-start | bytes 1572872 | tf_op jit(solution)/shard_map/while/body/eval_jaxpr/cond/branch_2_fun/ppermute | solution.py:369
  196.9 2.1 collective-permute-start.39
  199.7 25.7 %collective-permute-start.40 = (bf16[2048,128]{1,0:T(8,128)(2,1)S(1)}, bf16[2048,128]{1,0:T(8,128)(2,1)}, u32[]{:S(2)}, u32[]{:S(2)}) collective-permute-start(bf16[2048,128]{1,0:T(8,128)(2,1)S(1)} %get-tuple-element.463), channel_id=1, source_target_pairs={{0,4},{4,0},{1,5},{5,1},{2,10},{6,14},{3,7},{7,3},{8,9},{12,13},{9... | collective-permute-start | bytes 1572872 | tf_op jit(solution)/shard_map/while/body/eval_jaxpr/cond/branch_9_fun/ppermute | solution.py:369
  211.1 14.3 %collective-permute-start.41 = (bf16[2048,128]{1,0:T(8,128)(2,1)S(1)}, bf16[2048,128]{1,0:T(8,128)(2,1)}, u32[]{:S(2)}, u32[]{:S(2)}) collective-permute-start(bf16[2048,128]{1,0:T(8,128)(2,1)S(1)} %get-tuple-element.464), channel_id=1, source_target_pairs={{0,4},{4,0},{1,5},{5,1},{2,6},{6,2},{3,7},{7,3},{8,12},{12,8},{9,1... | collective-permute-start | bytes 1572872 | tf_op jit(solution)/shard_map/while/body/eval_jaxpr/cond/branch_9_fun/ppermute | solution.py:369
  229.1 35.9 %collective-permute-start.29 = (bf16[2048,128]{1,0:T(8,128)(2,1)S(1)}, bf16[2048,128]{1,0:T(8,128)(2,1)}, u32[]{:S(2)}, u32[]{:S(2)}) collective-permute-start(bf16[2048,128]{1,0:T(8,128)(2,1)S(1)} %param.9), channel_id=1, source_target_pairs={{0,4},{4,0},{1,5},{5,1},{2,6},{6,2},{3,7},{7,3},{8,12},{12,8},{9,2... | collective-permute-start | bytes 1572872 | tf_op jit(solution)/shard_map/while/body/eval_jaxpr/cond/branch_5_fun/ppermute | solution.py:369
  253.5 11.5 %collective-permute-start.28 = (bf16[2048,128]{1,0:T(8,128)(2,1)S(1)}, bf16[2048,128]{1,0:T(8,128)(2,1)}, u32[]{:S(2)}, u32[]{:S(2)}) collective-permute-start(bf16[2048,128]{1,0:T(8,128)(2,1)S(1)} %param.9), channel_id=1, source_target_pairs={{0,4},{4,0},{1,5},{5,1},{2,6},{6,2},{3,7},{7,3},{8,12},{12,8},{9,1... | collective-permute-start | bytes 1572872 | tf_op jit(solution)/shard_map/while/body/eval_jaxpr/cond/branch_5_fun/ppermute | solution.py:369
  259.2 29.0 %collective-permute-start.27 = (bf16[2048,128]{1,0:T(8,128)(2,1)S(1)}, bf16[2048,128]{1,0:T(8,128)(2,1)}, u32[]{:S(2)}, u32[]{:S(2)}) collective-permute-start(bf16[2048,128]{1,0:T(8,128)(2,1)S(1)} %param.9), channel_id=1, source_target_pairs={{0,4},{4,0},{1,8},{5,12},{2,6},{6,2},{3,7},{7,3},{8,9},{12,13},{9,... | collective-permute-start | bytes 1572872 | tf_op jit(solution)/shard_map/while/body/eval_jaxpr/cond/branch_5_fun/ppermute | solution.py:369
  291.1 15.0 %collective-permute-start.33 = (bf16[2048,128]{1,0:T(8,128)(2,1)S(1)}, bf16[2048,128]{1,0:T(8,128)(2,1)}, u32[]{:S(2)}, u32[]{:S(2)}) collective-permute-start(bf16[2048,128]{1,0:T(8,128)(2,1)S(1)} %get-tuple-element.438.pay), channel_id=1, source_target_pairs={{0,4},{4,0},{1,5},{5,1},{2,6},{6,2},{3,7},{7,3},{8,12},{12,8},{9,2... | collective-permute-start | bytes 1572872 | tf_op jit(solution)/shard_map/while/body/eval_jaxpr/cond/branch_7_fun/ppermute | solution.py:369
  306.7 21.7 %collective-permute-start.34 = (bf16[2048,128]{1,0:T(8,128)(2,1)S(1)}, bf16[2048,128]{1,0:T(8,128)(2,1)}, u32[]{:S(2)}, u32[]{:S(2)}) collective-permute-start(bf16[2048,128]{1,0:T(8,128)(2,1)S(1)} %get-tuple-element.445), channel_id=1, source_target_pairs={{0,4},{4,0},{1,5},{5,1},{2,6},{6,2},{3,7},{7,3},{8,12},{12,8},{9,1... | collective-permute-start | bytes 1572872 | tf_op jit(solution)/shard_map/while/body/eval_jaxpr/cond/branch_7_fun/ppermute | solution.py:369
  307.2 23.0 %collective-permute-start.35 = (bf16[2048,128]{1,0:T(8,128)(2,1)S(1)}, bf16[2048,128]{1,0:T(8,128)(2,1)}, u32[]{:S(2)}, u32[]{:S(2)}) collective-permute-start(bf16[2048,128]{1,0:T(8,128)(2,1)S(1)} %get-tuple-element.446), channel_id=1, source_target_pairs={{0,4},{4,0},{1,9},{5,13},{2,6},{6,2},{3,7},{7,3},{8,12},{12,8},{9,... | collective-permute-start | bytes 1572872 | tf_op jit(solution)/shard_map/while/body/eval_jaxpr/cond/branch_7_fun/ppermute | solution.py:369
  335.8 2.1 collective-permute-start.49
  336.2 2.4 collective-permute-start.50
  341.5 61.6 %collective-permute-start.21 = (bf16[2048,128]{1,0:T(8,128)(2,1)S(1)}, bf16[2048,128]{1,0:T(8,128)(2,1)}, u32[]{:S(2)}, u32[]{:S(2)}) collective-permute-start(bf16[2048,128]{1,0:T(8,128)(2,1)S(1)} %get-tuple-element.412.pay), channel_id=1, source_target_pairs={{0,24},{4,28},{1,5},{5,1},{2,6},{6,2},{3,7},{7,3},{8,12},{12,8},{9... | collective-permute-start | bytes 1572872 | tf_op jit(solution)/shard_map/while/body/eval_jaxpr/cond/branch_3_fun/ppermute | solution.py:369
  403.7 25.8 %collective-permute-start.22 = (bf16[2048,128]{1,0:T(8,128)(2,1)S(1)}, bf16[2048,128]{1,0:T(8,128)(2,1)}, u32[]{:S(2)}, u32[]{:S(2)}) collective-permute-start(bf16[2048,128]{1,0:T(8,128)(2,1)S(1)} %get-tuple-element.419), channel_id=1, source_target_pairs={{0,4},{4,0},{1,5},{5,1},{2,6},{6,2},{3,7},{7,3},{8,12},{12,8},{9,1... | collective-permute-start | bytes 1572872 | tf_op jit(solution)/shard_map/while/body/eval_jaxpr/cond/branch_3_fun/ppermute | solution.py:369
  423.7 18.4 %collective-permute-start.23 = (bf16[2048,128]{1,0:T(8,128)(2,1)S(1)}, bf16[2048,128]{1,0:T(8,128)(2,1)}, u32[]{:S(2)}, u32[]{:S(2)}) collective-permute-start(bf16[2048,128]{1,0:T(8,128)(2,1)S(1)} %get-tuple-element.420), channel_id=1, source_target_pairs={{0,8},{4,12},{1,5},{5,1},{2,6},{6,2},{3,7},{7,3},{8,0},{12,4},{9,1... | collective-permute-start | bytes 1572872 | tf_op jit(solution)/shard_map/while/body/eval_jaxpr/cond/branch_3_fun/ppermute | solution.py:369
  455.7 29.4 %collective-permute-start.59 = (bf16[2048,128]{1,0:T(8,128)(2,1)S(1)}, bf16[2048,128]{1,0:T(8,128)(2,1)}, u32[]{:S(2)}, u32[]{:S(2)}) collective-permute-start(bf16[2048,128]{1,0:T(8,128)(2,1)S(1)} %param.19), channel_id=1, source_target_pairs={{0,4},{4,0},{1,5},{5,1},{2,6},{6,2},{3,7},{7,3},{8,12},{12,8},{9,1... | collective-permute-start | bytes 1572872 | tf_op jit(solution)/shard_map/while/body/eval_jaxpr/cond/branch_15_fun/ppermute | solution.py:369
  455.8 29.4 %collective-permute-start.58 = (bf16[2048,128]{1,0:T(8,128)(2,1)S(1)}, bf16[2048,128]{1,0:T(8,128)(2,1)}, u32[]{:S(2)}, u32[]{:S(2)}) collective-permute-start(bf16[2048,128]{1,0:T(8,128)(2,1)S(1)} %param.19), channel_id=1, source_target_pairs={{0,4},{4,0},{1,5},{5,1},{2,6},{6,2},{3,7},{7,3},{8,12},{12,8},{9,1... | collective-permute-start | bytes 1572872 | tf_op jit(solution)/shard_map/while/body/eval_jaxpr/cond/branch_15_fun/ppermute | solution.py:369
  479.4 7.4 %collective-permute-start.57 = (bf16[2048,128]{1,0:T(8,128)(2,1)S(1)}, bf16[2048,128]{1,0:T(8,128)(2,1)}, u32[]{:S(2)}, u32[]{:S(2)}) collective-permute-start(bf16[2048,128]{1,0:T(8,128)(2,1)S(1)} %param.19), channel_id=1, source_target_pairs={{0,4},{4,0},{1,5},{5,1},{2,6},{6,2},{3,24},{7,28},{8,12},{12,8},{9... | collective-permute-start | bytes 1572872 | tf_op jit(solution)/shard_map/while/body/eval_jaxpr/cond/branch_15_fun/ppermute | solution.py:369
  487.5 2.7 collective-permute-start.65
  492.6 55.1 %all-to-all-start = ((f32[4,2,512,128]{3,2,1,0:T(8,128)}), f32[4,2,512,128]{3,2,1,0:T(8,128)S(1)}, u32[]{:S(2)}, u32[]{:S(2)}) async-start(f32[4,2,512,128]{3,2,1,0:T(8,128)} %copy.37), calls=%async_computation | async-start | bytes 4194304 | tf_op jit(solution)/shard_map/all_to_all | solution.py:463
  (15 other events, 100.2 us)
